TPU v7x, 32 devices: a whole 2x2x4 slice. The times are simulated.
32 devices in a mesh: vid: 2 (over core), txt: 4 (over y, x), head: 4 (over z).
Axes of the slice: x: 2, y: 2, z: 4, core: 2. Of those that a mesh axis runs over, the one named last changes fastest.
Arguments:
- latents: bfloat16 [32, 128, 768], P('txt', 'vid'), may hold values from -6 to 6
- video_tokens: bfloat16 [32, 1024, 768], P('txt', 'vid'), may hold values from -6 to 6
- caption_tokens: bfloat16 [32, 64, 768], P('vid', 'txt'), may hold values from -6 to 6
- caption_len: int32 [32], P('vid'), may hold values from 5 to 60
- key_mask: int32 [32, 64], P('vid', 'txt'), may hold values 0 or 1
- drop_flags: int32 [32], P('txt'), may hold values 0 or 1
- gain_latent: float32 [768], replicated, may hold values from 0.5 to 1.5
- gain_tokens: float32 [768], replicated, may hold values from 0.5 to 1.5
- gain_mlp: float32 [768], replicated, may hold values from 0.5 to 1.5
- query_weight: bfloat16 [768, 768], P(None, 'head'), may hold values from -0.21875 to 0.21875
- key_matrix: bfloat16 [768, 768], P(None, 'head'), may hold values from -0.21875 to 0.21875
- value_matrix: bfloat16 [768, 768], P(None, 'head'), may hold values from -0.21875 to 0.21875
- out_weight: bfloat16 [768, 768], P('head'), may hold values from -6 to 6
- up_weight: bfloat16 [768, 3072], P(None, 'head'), may hold values from -0.21875 to 0.21875
- down_weight: bfloat16 [3072, 768], P('head'), may hold values from -0.109375 to 0.109375
- cotangent: bfloat16 [32, 128, 768], P('txt', 'vid'), may hold values from -6 to 6
Outputs:
- latents_out: bfloat16 [32, 128, 768], P('txt', 'vid')
- latent_grad: float32 [32, 128, 768], P('txt', 'vid')
- video_grad: float32 [32, 1024, 768], P('txt', 'vid')
- caption_grad: float32 [32, 64, 768], P('vid', 'txt')
- grad_query: float32 [768, 768], P(None, 'head')
- grad_key: float32 [768, 768], P(None, 'head')
- grad_value: float32 [768, 768], P(None, 'head')
- grad_out: float32 [768, 768], P('head')
- grad_up: float32 [768, 3072], P(None, 'head')
- grad_down: float32 [3072, 768], P('head')
- grad_gain_latent: float32 [768], replicated
- grad_gain_tokens: float32 [768], replicated
- grad_gain_mlp: float32 [768], replicated
- kept_count: int32 [], replicated
All inputs are finite; a program needn't handle non-finite values. No bound on the sum of `key_mask` or of `drop_flags` on one device may be relied on, other than what follows from the above.
Results may differ from a plain program's by a relative error of at most 0.012.
Values may be sent and summed in bfloat16 or wider, within the bound.
No kernel may reach another device: no remote copies, remote signals or barrier semaphores. Data moves between devices by JAX's collectives and lax.ppermute only.
A program may use at most 128 MiB of HBM per device.

v0:
```python
import math

import jax
import jax.numpy as jnp
from jax import lax
from jax.sharding import PartitionSpec as P

D = 768
HEADS = 12


def combined_all(part, axis, combine):
    gathered = jax.tree.map(lambda a: lax.all_gather(a, axis), part)

    def take(source):
        return jax.tree.map(lambda a: lax.dynamic_index_in_dim(a, source, 0, False), gathered)

    return lax.fori_loop(
        1, lax.axis_size(axis), lambda source, state: combine(state, take(source)), take(0)
    )


def layer_norm(values, gain):
    center = values - jnp.mean(values, axis=-1, keepdims=True)
    spread = jnp.mean(center * center, axis=-1, keepdims=True)
    return center * lax.rsqrt(spread + 1e-05) * gain


def norm_back(values, gain, upstream):
    result, pullback = jax.vjp(layer_norm, values, gain)
    return pullback(upstream)


def gelu_exact(values):
    return jax.nn.gelu(values, approximate=False)


def combine_stats(first, second):
    peak = jnp.maximum(first[0], second[0])
    total = first[1] * jnp.exp(first[0] - peak) + second[1] * jnp.exp(second[0] - peak)
    return (peak, total)


def to_blocks(whole, vid_count, txt_count):
    items, rows, width = whole.shape
    split = whole.reshape(txt_count, items // txt_count, vid_count, rows // vid_count, width)
    return split.transpose(2, 0, 1, 3, 4).reshape(
        vid_count * txt_count, items // txt_count, rows // vid_count, width
    )


def from_blocks(blocked, vid_count, txt_count):
    count, items_here, rows_here, width = blocked.shape
    split = blocked.reshape(vid_count, txt_count, items_here, rows_here, width)
    return split.transpose(1, 2, 0, 3, 4).reshape(
        txt_count * items_here, vid_count * rows_here, width
    )


def place_sum(whole, part, start):
    current = lax.dynamic_slice_in_dim(whole, start, part.shape[0], 0)
    return lax.dynamic_update_slice_in_dim(whole, current + part, start, 0)


def place_stats(peak_all, total_all, peak, total, start):
    old_peak = lax.dynamic_slice_in_dim(peak_all, start, peak.shape[0], 0)
    old_total = lax.dynamic_slice_in_dim(total_all, start, peak.shape[0], 0)
    new_peak, new_total = combine_stats((old_peak, old_total), (peak, total))
    peak_all = lax.dynamic_update_slice_in_dim(peak_all, new_peak, start, 0)
    total_all = lax.dynamic_update_slice_in_dim(total_all, new_total, start, 0)
    return (peak_all, total_all)


def take_rows(whole, start, count):
    return lax.dynamic_slice_in_dim(whole, start, count, 0)


def local(
    latents,
    video_tokens,
    caption_tokens,
    caption_len,
    key_mask,
    drop_flags,
    gain_latent,
    gain_tokens,
    gain_mlp,
    query_weight,
    key_matrix,
    value_matrix,
    out_weight,
    up_weight,
    down_weight,
    cotangent,
):
    vid_count = lax.axis_size("vid")
    txt_count = lax.axis_size("txt")
    vid_index = lax.axis_index("vid")
    txt_index = lax.axis_index("txt")
    items_here = latents.shape[0]
    cap_items = caption_tokens.shape[0]
    items_total = items_here * txt_count
    head_width = query_weight.shape[1]
    head_size = D // HEADS
    heads_here = head_width // head_size
    scale = 1.0 / math.sqrt(head_size)
    video_here = video_tokens.shape[1]
    cap_here = caption_tokens.shape[1]
    video_start = txt_index * items_here
    cap_start = vid_index * cap_items
    keep = (1 - drop_flags).astype(jnp.float32)
    slots = txt_index * cap_here + jnp.arange(cap_here, dtype=jnp.int32)
    cap_valid = (slots[None, :] < caption_len[:, None]) & (key_mask == 1)
    cap_mask = cap_valid[:, None, None, :]

    def split_heads(values):
        return values.reshape(values.shape[0], values.shape[1], heads_here, head_size)

    lat_float = latents.astype(jnp.float32)
    lat_norm = layer_norm(lat_float, gain_latent).astype(jnp.bfloat16)
    queries = jnp.einsum(
        "bld,de->ble", lat_norm, query_weight, preferred_element_type=jnp.float32
    ).astype(jnp.bfloat16)
    all_queries = from_blocks(
        lax.all_gather(queries[None], ("vid", "txt"), axis=0, tiled=True), vid_count, txt_count
    )
    lat_total = all_queries.shape[1]
    video_queries = take_rows(all_queries, video_start, items_here)
    cap_queries = take_rows(all_queries, cap_start, cap_items)
    video_float = video_tokens.astype(jnp.float32)
    cap_float = caption_tokens.astype(jnp.float32)
    video_normed = layer_norm(video_float, gain_tokens).astype(jnp.bfloat16)
    caption_normed = layer_norm(cap_float, gain_tokens).astype(jnp.bfloat16)
    video_keys = jnp.einsum(
        "flc,co->flo", video_normed, key_matrix, preferred_element_type=jnp.float32
    ).astype(jnp.bfloat16)
    video_values = jnp.einsum(
        "flc,co->flo", video_normed, value_matrix, preferred_element_type=jnp.float32
    ).astype(jnp.bfloat16)
    cap_keys = jnp.einsum(
        "flc,co->flo", caption_normed, key_matrix, preferred_element_type=jnp.float32
    ).astype(jnp.bfloat16)
    cap_values = jnp.einsum(
        "flc,co->flo", caption_normed, value_matrix, preferred_element_type=jnp.float32
    ).astype(jnp.bfloat16)
    video_scores = (
        jnp.einsum(
            "blhe,bkhe->bhlk",
            split_heads(video_queries),
            split_heads(video_keys),
            preferred_element_type=jnp.float32,
        )
        * scale
    )
    cap_scores = (
        jnp.einsum(
            "blhe,bkhe->bhlk",
            split_heads(cap_queries),
            split_heads(cap_keys),
            preferred_element_type=jnp.float32,
        )
        * scale
    )
    cap_scores = jnp.where(cap_mask, cap_scores, -1e30)
    video_peak = jnp.max(video_scores, axis=-1)
    video_total = jnp.sum(jnp.exp(video_scores - video_peak[..., None]), axis=-1)
    cap_peak = jnp.max(cap_scores, axis=-1)
    cap_total = jnp.sum(
        jnp.where(cap_mask, jnp.exp(cap_scores - cap_peak[..., None]), 0.0), axis=-1
    )
    peak_all = jnp.full((items_total, heads_here, lat_total), -1e30, jnp.float32)
    total_all = jnp.zeros((items_total, heads_here, lat_total), jnp.float32)
    peak_all, total_all = place_stats(peak_all, total_all, video_peak, video_total, video_start)
    peak_all, total_all = place_stats(peak_all, total_all, cap_peak, cap_total, cap_start)
    peak, total = combined_all((peak_all, total_all), ("vid", "txt"), combine_stats)
    video_probs = (
        jnp.exp(video_scores - take_rows(peak, video_start, items_here)[..., None])
        / take_rows(total, video_start, items_here)[..., None]
    )
    cap_probs = jnp.where(
        cap_mask,
        jnp.exp(cap_scores - take_rows(peak, cap_start, cap_items)[..., None])
        / take_rows(total, cap_start, cap_items)[..., None],
        0.0,
    )
    video_low = video_probs.astype(jnp.bfloat16)
    cap_low = cap_probs.astype(jnp.bfloat16)
    video_part = jnp.einsum(
        "bhlk,bkhe->blhe", video_low, split_heads(video_values), preferred_element_type=jnp.float32
    ).reshape(items_here, lat_total, head_width)
    cap_part = jnp.einsum(
        "bhlk,bkhe->blhe", cap_low, split_heads(cap_values), preferred_element_type=jnp.float32
    ).reshape(cap_items, lat_total, head_width)
    value_all = jnp.zeros((items_total, lat_total, head_width), jnp.float32)
    value_all = place_sum(place_sum(value_all, video_part, video_start), cap_part, cap_start)
    attended = lax.psum_scatter(
        to_blocks(value_all, vid_count, txt_count), ("vid", "txt"), scatter_dimension=0, tiled=True
    )[0]
    mixed_in = (attended * keep[:, None, None]).astype(jnp.bfloat16)
    branch = lax.psum(
        jnp.einsum("ble,ed->bld", mixed_in, out_weight, preferred_element_type=jnp.float32), "head"
    )
    after_attn = lat_float + branch
    mlp_norm = layer_norm(after_attn, gain_mlp).astype(jnp.bfloat16)
    pre_act = jnp.einsum("bld,df->blf", mlp_norm, up_weight, preferred_element_type=jnp.float32)
    activ = gelu_exact(pre_act).astype(jnp.bfloat16)
    growth = lax.psum(
        jnp.einsum("blf,fd->bld", activ, down_weight, preferred_element_type=jnp.float32).astype(
            jnp.bfloat16
        ),
        "head",
    ).astype(jnp.float32)
    latents_out = (after_attn + growth).astype(jnp.bfloat16)
    grad_down = jnp.einsum("blf,bld->fd", activ, cotangent, preferred_element_type=jnp.float32)
    d_activ = jnp.einsum("bld,fd->blf", cotangent, down_weight, preferred_element_type=jnp.float32)
    d_pre = jax.vjp(gelu_exact, pre_act)[1](d_activ)[0].astype(jnp.bfloat16)
    grad_up = jnp.einsum("bld,blf->df", mlp_norm, d_pre, preferred_element_type=jnp.float32)
    d_mlp_norm = lax.psum(
        jnp.einsum("blf,df->bld", d_pre, up_weight, preferred_element_type=jnp.float32), "head"
    )
    d_after_norm, grad_gain_mlp = norm_back(after_attn, gain_mlp, d_mlp_norm)
    d_after = cotangent.astype(jnp.float32) + d_after_norm
    d_branch = d_after.astype(jnp.bfloat16)
    grad_out = jnp.einsum("ble,bld->ed", mixed_in, d_branch, preferred_element_type=jnp.float32)
    d_att = (
        jnp.einsum("bld,ed->ble", d_branch, out_weight, preferred_element_type=jnp.float32)
        * keep[:, None, None]
    ).astype(jnp.bfloat16)
    all_d_att = from_blocks(
        lax.all_gather(d_att[None], ("vid", "txt"), axis=0, tiled=True), vid_count, txt_count
    )
    video_d_att = split_heads(take_rows(all_d_att, video_start, items_here))
    cap_d_att = split_heads(take_rows(all_d_att, cap_start, cap_items))
    video_dprobs = jnp.einsum(
        "blhe,bkhe->bhlk",
        video_d_att,
        split_heads(video_values),
        preferred_element_type=jnp.float32,
    )
    cap_dprobs = jnp.einsum(
        "blhe,bkhe->bhlk", cap_d_att, split_heads(cap_values), preferred_element_type=jnp.float32
    )
    delta_all = jnp.zeros((items_total, heads_here, lat_total), jnp.float32)
    delta_all = place_sum(delta_all, jnp.sum(video_probs * video_dprobs, axis=-1), video_start)
    delta_all = place_sum(delta_all, jnp.sum(cap_probs * cap_dprobs, axis=-1), cap_start)
    delta = lax.psum(delta_all, ("vid", "txt"))
    video_dscores = (
        video_probs * (video_dprobs - take_rows(delta, video_start, items_here)[..., None])
    ).astype(jnp.bfloat16)
    cap_dscores = (
        cap_probs * (cap_dprobs - take_rows(delta, cap_start, cap_items)[..., None])
    ).astype(jnp.bfloat16)
    video_dq = (
        jnp.einsum(
            "bhlk,bkhe->blhe",
            video_dscores,
            split_heads(video_keys),
            preferred_element_type=jnp.float32,
        )
        * scale
    ).reshape(items_here, lat_total, head_width)
    cap_dq = (
        jnp.einsum(
            "bhlk,bkhe->blhe",
            cap_dscores,
            split_heads(cap_keys),
            preferred_element_type=jnp.float32,
        )
        * scale
    ).reshape(cap_items, lat_total, head_width)
    query_all = jnp.zeros((items_total, lat_total, head_width), jnp.float32)
    query_all = place_sum(place_sum(query_all, video_dq, video_start), cap_dq, cap_start)
    d_queries = lax.psum_scatter(
        to_blocks(query_all, vid_count, txt_count), ("vid", "txt"), scatter_dimension=0, tiled=True
    )[0].astype(jnp.bfloat16)
    video_key_grad = (
        (
            jnp.einsum(
                "bhlk,blhe->bkhe",
                video_dscores,
                split_heads(video_queries),
                preferred_element_type=jnp.float32,
            )
            * scale
        )
        .reshape(items_here, video_here, head_width)
        .astype(jnp.bfloat16)
    )
    video_value_grad = (
        jnp.einsum("bhlk,blhe->bkhe", video_low, video_d_att, preferred_element_type=jnp.float32)
        .reshape(items_here, video_here, head_width)
        .astype(jnp.bfloat16)
    )
    caption_key_grad = (
        (
            jnp.einsum(
                "bhlk,blhe->bkhe",
                cap_dscores,
                split_heads(cap_queries),
                preferred_element_type=jnp.float32,
            )
            * scale
        )
        .reshape(cap_items, cap_here, head_width)
        .astype(jnp.bfloat16)
    )
    caption_value_grad = (
        jnp.einsum("bhlk,blhe->bkhe", cap_low, cap_d_att, preferred_element_type=jnp.float32)
        .reshape(cap_items, cap_here, head_width)
        .astype(jnp.bfloat16)
    )
    grad_query = jnp.einsum("bld,ble->de", lat_norm, d_queries, preferred_element_type=jnp.float32)
    d_lat_norm = lax.psum(
        jnp.einsum("ble,de->bld", d_queries, query_weight, preferred_element_type=jnp.float32),
        "head",
    )
    d_lat_back, grad_gain_latent = norm_back(lat_float, gain_latent, d_lat_norm)
    latent_grad = d_after + d_lat_back
    grad_key = jnp.einsum(
        "zsg,zsv->gv", video_normed, video_key_grad, preferred_element_type=jnp.float32
    ) + jnp.einsum(
        "zsg,zsv->gv", caption_normed, caption_key_grad, preferred_element_type=jnp.float32
    )
    grad_value = jnp.einsum(
        "zsg,zsv->gv", video_normed, video_value_grad, preferred_element_type=jnp.float32
    ) + jnp.einsum(
        "zsg,zsv->gv", caption_normed, caption_value_grad, preferred_element_type=jnp.float32
    )
    video_term = jnp.einsum(
        "ayt,ot->ayo", video_key_grad, key_matrix, preferred_element_type=jnp.float32
    ) + jnp.einsum(
        "ayt,ot->ayo", video_value_grad, value_matrix, preferred_element_type=jnp.float32
    )
    cap_term = jnp.einsum(
        "ayt,ot->ayo", caption_key_grad, key_matrix, preferred_element_type=jnp.float32
    ) + jnp.einsum(
        "ayt,ot->ayo", caption_value_grad, value_matrix, preferred_element_type=jnp.float32
    )
    d_video_norm, d_cap_norm = lax.psum((video_term, cap_term), "head")
    video_grad, video_gain_part = norm_back(video_float, gain_tokens, d_video_norm)
    caption_grad, cap_gain_part = norm_back(cap_float, gain_tokens, d_cap_norm)
    grad_gain_tokens = video_gain_part + cap_gain_part
    kept_here = jnp.sum(keep)
    (
        grad_query,
        grad_key,
        grad_value,
        grad_out,
        grad_up,
        grad_down,
        grad_gain_latent,
        grad_gain_tokens,
        grad_gain_mlp,
        kept_total,
    ) = lax.psum(
        (
            grad_query,
            grad_key,
            grad_value,
            grad_out,
            grad_up,
            grad_down,
            grad_gain_latent,
            grad_gain_tokens,
            grad_gain_mlp,
            kept_here,
        ),
        ("vid", "txt"),
    )
    kept_count = (kept_total / vid_count).astype(jnp.int32)
    return (
        latents_out,
        latent_grad,
        video_grad,
        caption_grad,
        grad_query,
        grad_key,
        grad_value,
        grad_out,
        grad_up,
        grad_down,
        grad_gain_latent,
        grad_gain_tokens,
        grad_gain_mlp,
        kept_count,
    )


def solution(mesh):
    in_specs = (
        P("txt", "vid", None),
        P("txt", "vid", None),
        P("vid", "txt", None),
        P("vid"),
        P("vid", "txt"),
        P("txt"),
        P(),
        P(),
        P(),
        P(None, "head"),
        P(None, "head"),
        P(None, "head"),
        P("head", None),
        P(None, "head"),
        P("head", None),
        P("txt", "vid", None),
    )
    out_specs = (
        P("txt", "vid", None),
        P("txt", "vid", None),
        P("txt", "vid", None),
        P("vid", "txt", None),
        P(None, "head"),
        P(None, "head"),
        P(None, "head"),
        P("head", None),
        P(None, "head"),
        P("head", None),
        P(),
        P(),
        P(),
        P(),
    )
    return jax.shard_map(local, mesh=mesh, in_specs=in_specs, out_specs=out_specs, check_vma=False)
```

profile of v0, /device:TPU:0, one launch (start us, length us, event | category | flops | bytes accessed | tf_op | source)
XLA Modules:
  0.0 1152.3 jit_solution(121106021653798068)
XLA Ops:
  19.3 4.8 fusion.13
  24.2 5.9 convolution_convert_fusion.1
  30.1 4.2 convolution_convert_fusion.2
  34.3 9.0 all-gather.5.cloned.1.call-done
  57.6 24.3 %all_gather.25 = f32[8,32,3,128]{3,1,2,0:T(8,128)S(1)} all-gather(f32[1,32,3,128]{3,1,2,0:T(8,128)S(1)} %copy.109), channel_id=1, replica_groups=mesh['vid'=2,'txt'=4,'head'=4] {'vid','txt'}, dimensions={0}, use_global_device_ids=true | all-gather | bytes 442368 | tf_op jit(solution)/shard_map/all_gather | solution.py:13
  81.9 24.5 %all_gather.28 = f32[8,32,3,128]{3,1,2,0:T(8,128)S(1)} all-gather(f32[1,32,3,128]{3,1,2,0:T(8,128)S(1)} %copy.110), channel_id=1, replica_groups=mesh['vid'=2,'txt'=4,'head'=4] {'vid','txt'}, dimensions={0}, use_global_device_ids=true | all-gather | bytes 442368 | tf_op jit(solution)/shard_map/all_gather | solution.py:13
  108.3 4.3 fusion.33
  123.6 51.8 %reduce-scatter.3.cloned.1.call-done = f32[1,8,64,192]{3,2,1,0:T(8,128)} async-done(((f32[8,8,64,192]{3,2,1,0:T(8,128)}), f32[1,8,64,192]{3,2,1,0:T(8,128)}) %reduce-scatter.3.cloned.1.call-update) | async-done | bytes 393232 | tf_op jit(solution)/shard_map/reduce_scatter | solution.py:196
  178.1 69.3 %all-reduce.9.cloned.1.call-done = f32[8,64,768]{2,1,0:T(8,128)} async-done(((f32[8,64,768]{2,1,0:T(8,128)}), f32[8,64,768]{2,1,0:T(8,128)}) %all-reduce.9.cloned.1.call-update) | async-done | bytes 1572880 | tf_op jit(solution)/shard_map/psum | solution.py:200
  251.3 4.2 multiply_convert_fusion.2
  263.8 64.1 %all-reduce.13.cloned.1.call-done = f32[8,64,768]{2,1,0:T(8,128)} async-done(((f32[8,64,768]{2,1,0:T(8,128)}), f32[8,64,768]{2,1,0:T(8,128)}) %all-reduce.13.cloned.1.call-update) | async-done | bytes 1572880 | tf_op jit(solution)/shard_map/psum | solution.py:218
  330.5 43.3 %all-reduce.11.cloned.1.call-done = bf16[8,64,768]{2,1,0:T(8,128)(2,1)} async-done(((bf16[8,64,768]{2,1,0:T(8,128)(2,1)}), bf16[8,64,768]{2,1,0:T(8,128)(2,1)}) %all-reduce.11.cloned.1.call-update) | async-done | bytes 786448 | tf_op jit(solution)/shard_map/psum | solution.py:207
  379.7 26.6 %all-gather.7.cloned.1.call-done = bf16[64,64,192]{2,1,0:T(8,128)(2,1)} async-done(((bf16[8,64,192]{2,1,0:T(8,128)(2,1)}), bf16[64,64,192]{2,1,0:T(8,128)(2,1)}) %all-gather.7.cloned.1.call-update) | async-done | bytes 1572880 | tf_op jit(solution)/shard_map/all_gather | solution.py:230
  410.7 5.8 multiply_reduce_fusion
  416.6 27.9 %psum.122 = f32[32,3,128]{2,1,0:T(4,128)S(1)} all-reduce(f32[32,3,128]{2,1,0:T(4,128)S(1)} %add_dynamic-update-slice_fusion.2), channel_id=1, replica_groups=mesh['vid'=2,'txt'=4,'head'=4] {'vid','txt'}, use_global_device_ids=true, to_apply=%region_22.23 | all-reduce | flops 12288 | bytes 98304 | tf_op jit(solution)/shard_map/psum | solution.py:246
  444.6 5.9 multiply_convert_fusion
  473.8 6.7 convolution_add_fusion
  480.5 32.0 %reduce-scatter.5.cloned.1.call-done = f32[1,8,64,192]{3,2,1,0:T(8,128)} async-done(((f32[8,8,64,192]{3,2,1,0:T(8,128)}), f32[1,8,64,192]{3,2,1,0:T(8,128)}) %reduce-scatter.5.cloned.1.call-update) | async-done | bytes 393232 | tf_op jit(solution)/shard_map/reduce_scatter | solution.py:273
  533.8 484.4 %all-reduce.17.cloned.1.call-done = (f32[8,64,768]{2,1,0:T(8,128)}, f32[8,512,768]{2,1,0:T(8,128)}, f32[16,16,768]{2,1,0:T(8,128)}) async-done(((f32[8,64,768]{2,1,0:T(8,128)}, f32[8,512,768]{2,1,0:T(8,128)}, f32[16,16,768]{2,1,0:T(8,128)}), (f32[8,64,768]{2,1,0:T(8,128)}, f32[8,512,768]{2,1,0:T(8,128)}, f32[16,16,768]{2,1,0:T(8,128)})) %all-reduce.17.cloned.1.call-update) | async-done | bytes 14942224 | tf_op jit(solution)/shard_map/psum | solution.py:313
  1019.6 10.1 fusion.14
  1032.2 6.6 fusion.12
  1040.7 28.1 %all-reduce = (f32[768]{0:T(1024)}, f32[768]{0:T(1024)}, f32[768]{0:T(1024)}, f32[]{:T(128)}) all-reduce(f32[768]{0:T(1024)S(1)} %get-tuple-element.163, f32[768]{0:T(1024)S(1)} %add.231, f32[768]{0:T(1024)S(1)} %copy-done.101, f32[]{:T(128)} %fusion.104), channel_id=1, replica_groups=mesh['vid'=2,'txt'=4,'head'=4] {'vid','txt'}, use_global_device_ids=true, to_apply=%region_40.41 | all-reduce | flops 2305 | bytes 18440 | tf_op jit(solution)/shard_map/psum | solution.py:355
  1075.5 10.8 broadcast_add_fusion
  1086.3 49.6 %all-reduce.15.cloned.1.call-done = (f32[768,192]{0,1:T(8,128)}, f32[768,192]{0,1:T(8,128)}, f32[768,192]{0,1:T(8,128)}, f32[192,768]{1,0:T(8,128)}, f32[768,768]{1,0:T(8,128)}, /*index=5*/f32[768,768]{1,0:T(8,128)}) async-done(((f32[768,192]{0,1:T(8,128)}, f32[768,192]{0,1:T(8,128)}, f32[768,192]{0,1:T(8,128)}, f32[192,768]{1,0:T(8,128)}, f32[768,768]{1,0:T(8,128)}, /*index=5*/f32[768,768]{1,0:T(8,128)}), ...) | async-done | bytes 7077904 | tf_op jit(solution)/shard_map/psum | solution.py:355
  (414 shorter events, 131.6 us)
Async XLA Ops:
  7.2 243.0 %copy-start = (bf16[768,768]{1,0:T(8,128)(2,1)S(1)}, bf16[768,768]{1,0:T(8,128)(2,1)}, u32[]{:S(2)}) copy-start(bf16[768,768]{1,0:T(8,128)(2,1)} %param.31) | copy-start | bytes 3538948
  7.2 36.0 %all-gather.5.cloned.1.call-start = ((), (), s32[]{:S(2)}) async-start(), calls=%async_computation.7 | async-start | bytes 2359296 | tf_op jit(solution)/shard_map/all_gather | solution.py:125
  12.6 162.8 %reduce-scatter.3.cloned.1.call-start = ((), (), s32[]{:S(2)}) async-start(), calls=%async_computation.2 | async-start | bytes 4718592 | tf_op jit(solution)/shard_map/reduce_scatter | solution.py:196
  19.1 36.4 %copy-start.32 = (bf16[16,16,3,64]{3,2,1,0:T(4,128)(2,1)}, bf16[16,16,3,64]{3,2,1,0:T(4,128)(2,1)S(1)}, u32[]{:S(2)}) copy-start(bf16[16,16,3,64]{3,2,1,0:T(4,128)(2,1)S(1)} %reshape.239) | copy-start | bytes 294916
  19.2 36.3 %copy-start.84 = (pred[16,16]{1,0:T(8,128)(4,1)}, pred[16,16]{1,0:T(8,128)(4,1)S(1)}, u32[]{:S(2)}) copy-start(pred[16,16]{1,0:T(8,128)(4,1)S(1)} %compare_and_fusion) | copy-start | bytes 772
  123.0 52.5 %copy-start.61 = (bf16[192,768]{1,0:T(8,128)(2,1)S(1)}, bf16[192,768]{1,0:T(8,128)(2,1)}, u32[]{:S(2)}) copy-start(bf16[192,768]{1,0:T(8,128)(2,1)} %param.30) | copy-start | bytes 884740
  123.0 124.4 %all-reduce.9.cloned.1.call-start = ((), (), s32[]{:S(2)}) async-start(), calls=%async_computation.3 | async-start | bytes 3145728 | tf_op jit(solution)/shard_map/psum | solution.py:200
  123.6 54.4 %copy-start.107 = (f32[8]{0:T(128)}, f32[8]{0:T(128)S(1)}, u32[]{:S(2)}) copy-start(f32[8]{0:T(128)S(1)} %subtract_convert_fusion) | copy-start | bytes 100
  178.1 149.8 %all-reduce.13.cloned.1.call-start = ((), (), s32[]{:S(2)}) async-start(), calls=%async_computation.5 | async-start | bytes 3145728 | tf_op jit(solution)/shard_map/psum | solution.py:218
  249.0 124.7 %copy-start.8 = (f32[8,64,768]{2,1,0:T(8,128)}, f32[8,64,768]{2,1,0:T(8,128)S(1)}, u32[]{:S(2)}) copy-start(f32[8,64,768]{2,1,0:T(8,128)S(1)} %get-tuple-element.199) | copy-start | bytes 4718596
  259.6 114.1 %all-reduce.11.cloned.1.call-start = ((), (), s32[]{:S(2)}) async-start(), calls=%async_computation.4 | async-start | bytes 1572864 | tf_op jit(solution)/shard_map/psum | solution.py:207
  260.7 67.2 %copy-start.82 = (f32[8,64]{1,0:T(8,128)S(1)}, f32[8,64]{1,0:T(8,128)}, u32[]{:S(2)}) copy-start(f32[8,64]{1,0:T(8,128)} %copy-done.81) | copy-start | bytes 6148
  260.7 67.2 %copy-start.99 = (f32[8,64]{1,0:T(8,128)S(1)}, f32[8,64]{1,0:T(8,128)}, u32[]{:S(2)}) copy-start(f32[8,64]{1,0:T(8,128)} %copy-done.98) | copy-start | bytes 6148
  260.7 67.2 %copy-start.103 = (f32[768]{0:T(1024)S(1)}, f32[768]{0:T(1024)}, u32[]{:S(2)}) copy-start(f32[768]{0:T(1024)} %param.26) | copy-start | bytes 9220
  263.7 66.7 %copy-start.97 = (f32[8,64]{1,0:T(8,128)S(1)}, f32[8,64]{1,0:T(8,128)}, u32[]{:S(2)}) copy-start(f32[8,64]{1,0:T(8,128)} %copy-done.96) | copy-start | bytes 6148
  263.8 142.5 %all-gather.7.cloned.1.call-start = ((), (), s32[]{:S(2)}) async-start(), calls=%async_computation.8 | async-start | bytes 2359296 | tf_op jit(solution)/shard_map/all_gather | solution.py:230
  378.0 30.0 %copy-start.45 = (bf16[8,64,768]{2,1,0:T(8,128)(2,1)}, bf16[8,64,768]{2,1,0:T(8,128)(2,1)S(1)}, u32[]{:S(2)}) copy-start(bf16[8,64,768]{2,1,0:T(8,128)(2,1)S(1)} %fusion.48) | copy-start | bytes 2359300
  379.1 133.4 %reduce-scatter.5.cloned.1.call-start = ((), (), s32[]{:S(2)}) async-start(), calls=%async_computation.6 | async-start | bytes 4718592 | tf_op jit(solution)/shard_map/reduce_scatter | solution.py:273
  461.2 557.0 %all-reduce.17.cloned.1.call-start = ((), (), s32[]{:S(2)}) async-start(), calls=%async_computation.10 | async-start | bytes 29884416 | tf_op jit(solution)/shard_map/psum | solution.py:313
  473.8 38.7 %copy-start.60 = (bf16[768,192]{0,1:T(8,128)(2,1)S(1)}, bf16[768,192]{0,1:T(8,128)(2,1)}, u32[]{:S(2)}) copy-start(bf16[768,192]{0,1:T(8,128)(2,1)} %param.27) | copy-start | bytes 884740
  515.1 620.9 %all-reduce.15.cloned.1.call-start = ((), (), s32[]{:S(2)}) async-start(), calls=%async_computation.9 | async-start | bytes 14155776 | tf_op jit(solution)/shard_map/psum | solution.py:355
  533.8 496.0 %slice-start.4 = ((s8[6291456]{0:T(1024)(128)(4,1)}), s8[2097152]{0:T(1024)(128)(4,1)S(1)}, s32[]{:S(2)}) async-start(s8[6291456]{0:T(1024)(128)(4,1)} %bitcast.180), calls=%async_computation.15 | async-start | bytes 4194304
  1039.4 36.1 %slice-start.6 = ((s8[6291456]{0:T(1024)(128)(4,1)}), s8[2097152]{0:T(1024)(128)(4,1)S(1)}, s32[]{:S(2)}) async-start(s8[6291456]{0:T(1024)(128)(4,1)} %bitcast.182), calls=%async_computation.17 | async-start | bytes 4194304
  1040.7 31.3 %copy-start.93 = (f32[8,64]{1,0:T(8,128)S(1)}, f32[8,64]{1,0:T(8,128)}, u32[]{:S(2)}) copy-start(f32[8,64]{1,0:T(8,128)} %copy-done.92) | copy-start | bytes 6148
  (111 other events, 322.7 us)
Sparse Core Ops, SparseCore 0:
  12.7 30.4 all-gather.4
  123.1 52.2 reduce-scatter.2
  178.4 68.9 all-reduce.8
  259.8 68.1 all-reduce.12
  330.7 42.9 all-reduce.10
  379.2 27.0 all-gather.6
  461.3 51.1 reduce-scatter.4
  515.9 502.2 all-reduce.16
  1023.4 112.5 all-reduce.14
where the time goes:
time: 1160 us; the launch traced here: 1150 us
  waiting for transfers between devices  830 us (72%)
  blocking collectives  105 us (9%)
  matrix products  73.1 us (6%)
  other arithmetic  71.9 us (6%)
  local copies, waits for them, and re-layouts  53.5 us (5%)
  between operations  17.5 us (2%)
    psum x1, waiting for transfers between devices, local(): lax.psum(jnp.einsum('ble,de->bld', d_queries, query_weight, preferred_ele...  484 us
    psum x1, waiting for transfers between devices, local(): lax.psum(jnp.einsum('ble,ed->bld', mixed_in, out_weight, preferred_elemen...  69.3 us
    psum x1, waiting for transfers between devices, local(): lax.psum(jnp.einsum('blf,df->bld', d_pre, up_weight, preferred_element_ty...  64.1 us
    reduce_scatter x1, waiting for transfers between devices, local(): lax.psum_scatter(to_blocks(value_all, vid_count, txt_count), ('vid', 'txt...  51.8 us
    psum x1, waiting for transfers between devices, local(): lax.psum((grad_query, grad_key, grad_value, grad_out, grad_up, grad_down,...  49.6 us
    all_gather x2, blocking collectives, combined_all(): gathered = jax.tree.map(lambda a: lax.all_gather(a, axis), part)  48.7 us
    psum x1, waiting for transfers between devices, local(): lax.psum(jnp.einsum('blf,fd->bld', activ, down_weight, preferred_element_...  43.3 us
    reduce_scatter x1, waiting for transfers between devices, local(): lax.psum_scatter(to_blocks(query_all, vid_count, txt_count), ('vid', 'txt...  32 us
  transfers between devices with their start and end apart: 9, of which 9 were waited for; matrix products, arithmetic and copies ran while one was open for 8% of the time, Pallas kernels for 0%

commit v1 on v0

--- a/solution.py
+++ b/solution.py
@@ -3,6 +3,8 @@
 import jax
 import jax.numpy as jnp
 from jax import lax
+from jax.experimental import pallas as pl
+from jax.experimental.pallas import tpu as pltpu
 from jax.sharding import PartitionSpec as P
 
 D = 768
@@ -75,7 +77,7 @@
     return lax.dynamic_slice_in_dim(whole, start, count, 0)
 
 
-def local(
+def local_general(
     latents,
     video_tokens,
     caption_tokens,
@@ -386,6 +388,501 @@
     )
 
 
+def swap_cores(values):
+    return lax.ppermute(values, "vid", [(0, 1), (1, 0)])
+
+
+def head_shift(values, shift, count):
+    return lax.ppermute(values, "head", [(i, (i - shift) % count) for i in range(count)])
+
+
+def take_block(values, index, size, axis=0):
+    return lax.dynamic_slice_in_dim(values, index * size, size, axis)
+
+
+def sum_over_head(part, place, count):
+    low = part.astype(jnp.bfloat16)
+    total = lax.dynamic_index_in_dim(part, place, 0, False)
+    for shift in range(1, count):
+        chunk = lax.dynamic_index_in_dim(low, (place - shift) % count, 0, False)
+        total = total + head_shift(chunk, shift, count).astype(jnp.float32)
+    total = total.astype(jnp.bfloat16)
+    result = lax.dynamic_update_index_in_dim(jnp.zeros_like(low), total, place, 0)
+    for shift in range(1, count):
+        result = lax.dynamic_update_index_in_dim(
+            result, head_shift(total, shift, count), (place + shift) % count, 0
+        )
+    return result
+
+
+def caption_perm(step, vid_count, txt_count, cores):
+    pairs = []
+    for v in range(vid_count):
+        for t in range(txt_count):
+            block = (t + step) % txt_count
+            dest_txt = v * (txt_count // vid_count) + block // cores
+            dest_vid = block % cores
+            pairs.append((v * txt_count + t, dest_vid * txt_count + dest_txt))
+    return pairs
+
+
+PAIR = 128
+F32 = jnp.float32
+BF16 = jnp.bfloat16
+
+
+def dot_nt(a, b):
+    return lax.dot_general(a, b, (((1,), (1,)), ((), ())), preferred_element_type=F32)
+
+
+def dot_nn(a, b):
+    return lax.dot_general(a, b, (((1,), (0,)), ((), ())), preferred_element_type=F32)
+
+
+def dot_tn(a, b):
+    return lax.dot_general(a, b, (((0,), (0,)), ((), ())), preferred_element_type=F32)
+
+
+def square(ref):
+    return ref[...].reshape(D, D)
+
+
+def two_heads(values):
+    low = lax.broadcasted_iota(jnp.int32, values.shape, 1) < PAIR // 2
+    zero = jnp.zeros_like(values)
+    return jnp.concatenate([jnp.where(low, values, zero), jnp.where(low, zero, values)], axis=0)
+
+
+def from_two_heads(both):
+    n = both.shape[1] // 2
+    first = lax.broadcasted_iota(jnp.int32, (PAIR, n), 0) < PAIR // 2
+    return jnp.where(first, both[:, :n], both[:, n:]).T
+
+
+def chunk_list(video, cap, size):
+    return [(start, size) for start in range(0, video, size)] + [(video, cap)]
+
+
+def norm_kernel(s_ref, own_ref, other_ref, cap_ref, gain_ref, out_ref):
+    gain = gain_ref[...]
+    start = 0
+    for ref in (own_ref, other_ref, cap_ref):
+        rows = ref.shape[0]
+        for at in range(0, rows, 64):
+            out_ref[pl.ds(start + at, 64), :] = layer_norm(
+                ref[pl.ds(at, 64), :].astype(F32), gain
+            ).astype(BF16)
+        start += rows
+
+
+def forward_kernel(
+    s_ref, tok_ref, lat_ref, mask_ref, wq_ref, wk_ref, wv_ref, wo_ref, gain_lat_ref, gain_mlp_ref,
+    q_ref, latn_ref, k_ref, v_ref, lse_ref, o_ref, mix_ref, after_ref, mlpn_ref, s_scr,
+):
+    item = pl.program_id(0)
+    lat = lat_ref[...].astype(F32)
+    latn = layer_norm(lat, gain_lat_ref[...]).astype(BF16)
+    latn_ref[...] = latn
+    q_ref[...] = (dot_nt(latn, square(wq_ref)).astype(BF16).astype(F32) * 0.125).astype(BF16)
+    keys = tok_ref.shape[0]
+    cap = mask_ref.shape[0]
+    step = keys // 4
+
+    def project(c, carry):
+        rows = pl.ds(pl.multiple_of(c * step, 16), step)
+        k_ref[rows, :] = dot_nt(tok_ref[rows, :], square(wk_ref)).astype(BF16)
+        v_ref[rows, :] = dot_nt(tok_ref[rows, :], square(wv_ref)).astype(BF16)
+        return carry
+
+    lax.fori_loop(0, 4, project, 0)
+    chunks = chunk_list(keys - cap, cap, 256)
+
+    def pair(p, carry):
+        cols = pl.ds(pl.multiple_of(p * PAIR, PAIR), PAIR)
+        q2 = two_heads(q_ref[:, cols])
+        peak = None
+        for start, size in chunks:
+            rows = pl.ds(start, size)
+            s = dot_nt(k_ref[rows, cols], q2)
+            if start == keys - cap:
+                mask = mask_ref[...]
+                s = jnp.where(jnp.concatenate([mask, mask], axis=1) > 0.5, s, -1e30)
+            s_scr[rows, :] = s
+            top = jnp.max(s, axis=0, keepdims=True)
+            peak = top if peak is None else jnp.maximum(peak, top)
+        total = jnp.zeros_like(peak)
+        out = jnp.zeros((PAIR, q2.shape[0]), F32)
+        for start, size in chunks:
+            rows = pl.ds(start, size)
+            e = jnp.exp(s_scr[rows, :] - peak)
+            total = total + jnp.sum(e, axis=0, keepdims=True)
+            out = out + dot_tn(v_ref[rows, cols], e.astype(BF16))
+        o_ref[:, cols] = from_two_heads(out / total)
+        lse_ref[pl.ds(p, 1), :] = peak + jnp.log(total)
+        return carry
+
+    lax.fori_loop(0, D // PAIR, pair, 0)
+    keep = (1 - s_ref[1 + item]).astype(F32)
+    mixed = (o_ref[...] * keep).astype(BF16)
+    mix_ref[...] = mixed
+    after = lat + dot_nn(mixed, square(wo_ref))
+    after_ref[...] = after
+    mlpn_ref[...] = layer_norm(after, gain_mlp_ref[...]).astype(BF16)
+
+
+def backward_kernel(
+    s_ref, q_ref, k_ref, v_ref, lse_ref, o_ref, datt_ref, own_ref, other_ref, cap_ref, mask_ref,
+    wk_ref, wv_ref, gain_ref,
+    dq_ref, dk_ref, dv_ref, own_out, other_out, cap_out, gain_out,
+):
+    item = pl.program_id(0)
+    keys = k_ref.shape[0]
+    cap = mask_ref.shape[0]
+    chunks = chunk_list(keys - cap, cap, 256)
+
+    def pair(p, carry):
+        cols = pl.ds(pl.multiple_of(p * PAIR, PAIR), PAIR)
+        q2 = two_heads(q_ref[:, cols])
+        d_att = datt_ref[:, cols]
+        d2 = two_heads(d_att)
+        prod = (d_att.astype(F32) * o_ref[:, cols]).T
+        delta = jnp.concatenate(
+            [
+                jnp.sum(prod[: PAIR // 2], axis=0, keepdims=True),
+                jnp.sum(prod[PAIR // 2 :], axis=0, keepdims=True),
+            ],
+            axis=1,
+        )
+        lse = lse_ref[pl.ds(p, 1), :]
+        dq = jnp.zeros((PAIR, q2.shape[0]), F32)
+        for start, size in chunks:
+            rows = pl.ds(start, size)
+            k = k_ref[rows, cols]
+            s = dot_nt(k, q2)
+            d_probs = dot_nt(v_ref[rows, cols], d2)
+            if start == keys - cap:
+                mask = mask_ref[...]
+                s = jnp.where(jnp.concatenate([mask, mask], axis=1) > 0.5, s, -1e30)
+            probs = jnp.exp(s - lse)
+            d_scores = (probs * (d_probs - delta)).astype(BF16)
+            dv_ref[rows, cols] = dot_nn(probs.astype(BF16), d2).astype(BF16)
+            dk_ref[rows, cols] = dot_nn(d_scores, q2).astype(BF16)
+            dq = dq + dot_tn(k, d_scores)
+        dq_ref[:, cols] = (from_two_heads(dq) * 0.125).astype(BF16)
+        return carry
+
+    lax.fori_loop(0, D // PAIR, pair, 0)
+    gain = gain_ref[...]
+
+    @pl.when(item == 0)
+    def _():
+        gain_out[...] = jnp.zeros_like(gain_out)
+
+    start = 0
+    for ref, out, size in ((own_ref, own_out, 256), (other_ref, other_out, 256), (cap_ref, cap_out, cap)):
+        def chunk(c, carry, ref=ref, out=out, size=size, start=start):
+            rows = pl.ds(pl.multiple_of(c * size, 16), size)
+            key_rows = pl.ds(pl.multiple_of(start + c * size, 16), size)
+            up = dot_nn(dk_ref[key_rows, :], square(wk_ref)) + dot_nn(
+                dv_ref[key_rows, :], square(wv_ref)
+            )
+            x = ref[rows, :].astype(F32)
+            center = x - jnp.mean(x, axis=-1, keepdims=True)
+            rate = lax.rsqrt(jnp.mean(center * center, axis=-1, keepdims=True) + 1e-05)
+            hat = center * rate
+            gain_out[pl.ds(0, 1), :] += jnp.sum(up * hat, axis=0, keepdims=True)
+            scaled = up * gain
+            first = jnp.mean(scaled, axis=-1, keepdims=True)
+            second = jnp.mean(scaled * hat, axis=-1, keepdims=True)
+            out[rows, :] = (rate * (scaled - first - hat * second)).astype(out.dtype)
+            return carry
+
+        lax.fori_loop(0, ref.shape[0] // size, chunk, 0)
+        start += ref.shape[0]
+
+
+def place_kernel(s_ref, whole_ref, part_ref, out_ref):
+    out_ref[...] = part_ref[...].astype(out_ref.dtype)
+
+
+def local(
+    latents,
+    video_tokens,
+    caption_tokens,
+    caption_len,
+    key_mask,
+    drop_flags,
+    gain_latent,
+    gain_tokens,
+    gain_mlp,
+    query_weight,
+    key_matrix,
+    value_matrix,
+    out_weight,
+    up_weight,
+    down_weight,
+    cotangent,
+):
+    txt_count = lax.axis_size("txt")
+    head_count = lax.axis_size("head")
+    core = lax.axis_index("vid")
+    place = lax.axis_index("txt")
+    z = lax.axis_index("head")
+    items_here = latents.shape[0]
+    own = items_here // 2
+    lat_half = latents.shape[1]
+    lat_rows = 2 * lat_half
+    video_here = video_tokens.shape[1]
+    cap_here = caption_tokens.shape[1]
+    cap_rows = cap_here * txt_count
+    keys_here = 2 * video_here + cap_rows
+    head_width = query_weight.shape[1]
+
+    def dot(spec, a, b):
+        return jnp.einsum(spec, a, b, preferred_element_type=F32)
+
+    packed = jnp.stack([query_weight.T, key_matrix.T, value_matrix.T, out_weight])
+    half = take_block(packed, core, 2)
+    mine = jnp.zeros((head_count,) + half.shape, BF16)
+    mine = lax.dynamic_update_index_in_dim(mine, half, z, 0)
+    for shift in range(1, head_count):
+        mine = lax.dynamic_update_index_in_dim(
+            mine, head_shift(half, shift, head_count), (z + shift) % head_count, 0
+        )
+    weights = jnp.zeros((2,) + mine.shape, BF16)
+    weights = lax.dynamic_update_index_in_dim(weights, mine, core, 0)
+    weights = lax.dynamic_update_index_in_dim(weights, swap_cores(mine), 1 - core, 0)
+
+    video_other = swap_cores(take_block(video_tokens, 1 - core, own))
+    both = jnp.concatenate([latents, cotangent], axis=1)
+    both_own = take_block(both, core, own)
+    both_other = swap_cores(take_block(both, 1 - core, own))
+    lat = jnp.concatenate([both_own[:, :lat_half], both_other[:, :lat_half]], axis=1)
+    cot = jnp.concatenate([both_own[:, lat_half:], both_other[:, lat_half:]], axis=1)
+    drop_own = take_block(drop_flags, core, own)
+    keep = (1 - drop_own).astype(F32)
+    scalars = jnp.concatenate([core[None].astype(jnp.int32), drop_own])
+
+    place_slots = place * cap_here + jnp.arange(cap_here, dtype=jnp.int32)
+    cap_valid = (place_slots[None, :] < caption_len[:, None]) & (key_mask == 1)
+    cap_flags = jnp.zeros((caption_tokens.shape[0], 1, D), BF16)
+    cap_flags = cap_flags.at[:, 0, :cap_here].set(cap_valid.astype(BF16))
+    cap_message = jnp.concatenate([caption_tokens, cap_flags], axis=1)
+    cap_parts = []
+    for step in range(txt_count):
+        block = take_block(cap_message, (place + step) % txt_count, own)
+        cap_parts.append(
+            lax.ppermute(block, ("vid", "txt"), caption_perm(step, 2, txt_count, 2))
+        )
+    cap = jnp.concatenate([part[:, :cap_here] for part in cap_parts], axis=1)
+    valid = jnp.concatenate([part[:, cap_here, :cap_here] for part in cap_parts], axis=1)
+    mask = jnp.broadcast_to(valid.astype(F32)[:, :, None], (own, cap_rows, lat_rows))
+
+    def item_spec(rows, width=D):
+        return pl.BlockSpec((None, rows, width), lambda i, s: (i, 0, 0))
+
+    def own_spec(rows):
+        return pl.BlockSpec((None, rows, D), lambda i, s: (s[0] * own + i, 0, 0))
+
+    def weight_spec(m):
+        return pl.BlockSpec(
+            (None, head_count, None, head_width, D),
+            lambda i, s: (m // 2, 0, m % 2, 0, 0),
+            pipeline_mode=pl.Buffered(1),
+        )
+
+    row_spec = pl.BlockSpec((1, D), lambda i, s: (0, 0))
+
+    def call(kernel, name, ins, outs, operands, scratch=(), aliases={}):
+        return pl.pallas_call(
+            kernel,
+            name=name,
+            grid_spec=pltpu.PrefetchScalarGridSpec(
+                num_scalar_prefetch=1,
+                grid=(own,),
+                in_specs=ins,
+                out_specs=[spec for spec, _, _ in outs],
+                scratch_shapes=list(scratch),
+            ),
+            out_shape=[jax.ShapeDtypeStruct(shape, dtype) for _, shape, dtype in outs],
+            input_output_aliases=aliases,
+            compiler_params=pltpu.CompilerParams(vmem_limit_bytes=56 << 20),
+        )(scalars, *operands)
+
+    def item_out(rows, dtype, width=D):
+        return (item_spec(rows, width), (own, rows, width), dtype)
+
+    gain_lat_row = gain_latent[None]
+    gain_tok_row = gain_tokens[None]
+    gain_mlp_row = gain_mlp[None]
+    (tok_norm,) = call(
+        norm_kernel,
+        "token_norm",
+        [own_spec(video_here), item_spec(video_here), item_spec(cap_rows), row_spec],
+        [item_out(keys_here, BF16)],
+        (video_tokens, video_other, cap, gain_tok_row),
+    )
+    queries, lat_norm, keys, values, lse, attended, mixed_in, after_attn, mlp_norm = call(
+        forward_kernel,
+        "attention_forward",
+        [item_spec(keys_here), item_spec(lat_rows), item_spec(cap_rows, lat_rows)]
+        + [weight_spec(m) for m in range(4)]
+        + [row_spec, row_spec],
+        [
+            item_out(lat_rows, BF16),
+            item_out(lat_rows, BF16),
+            item_out(keys_here, BF16),
+            item_out(keys_here, BF16),
+            item_out(8, F32, 2 * lat_rows),
+            item_out(lat_rows, F32),
+            item_out(lat_rows, BF16),
+            item_out(lat_rows, F32),
+            item_out(lat_rows, BF16),
+        ],
+        (tok_norm, lat, mask, weights, weights, weights, weights, gain_lat_row, gain_mlp_row),
+        [pltpu.VMEM((keys_here, 2 * lat_rows), F32)],
+    )
+
+    pre_act = dot("bld,df->blf", mlp_norm, up_weight)
+    activ, gelu_pull = jax.vjp(gelu_exact, pre_act)
+    activ = activ.astype(BF16)
+    d_pre = gelu_pull(dot("bld,fd->blf", cot, down_weight))[0].astype(BF16)
+    d_mlp_norm = sum_over_head(dot("blf,df->bld", d_pre, up_weight), z, head_count)
+    activ, d_mlp_norm = lax.optimization_barrier((activ, d_mlp_norm))
+    growth = lax.psum(dot("blf,fd->bld", activ, down_weight).astype(BF16), "head")
+    grad_down = dot("blf,bld->fd", activ, cot)
+    grad_up = dot("bld,blf->df", mlp_norm, d_pre)
+    out_mine = (after_attn + growth.astype(F32)).astype(BF16)
+
+    d_after_norm, gain_mlp_part = norm_back_rows(after_attn, gain_mlp, d_mlp_norm.astype(F32))
+    d_after = cot.astype(F32) + d_after_norm
+    d_branch = d_after.astype(BF16)
+    w_query = weights[0, :, 0].reshape(D, D)
+    w_out = weights[1, :, 1].reshape(D, D)
+    d_att = (dot("bld,ed->ble", d_branch, w_out) * keep[:, None, None]).astype(BF16)
+    d_queries, d_keys, d_values, video_grad, other_back, cap_back, gain_tok_part = call(
+        backward_kernel,
+        "attention_backward",
+        [
+            item_spec(lat_rows),
+            item_spec(keys_here),
+            item_spec(keys_here),
+            item_spec(8, 2 * lat_rows),
+            item_spec(lat_rows),
+            item_spec(lat_rows),
+            own_spec(video_here),
+            item_spec(video_here),
+            item_spec(cap_rows),
+            item_spec(cap_rows, lat_rows),
+            weight_spec(1),
+            weight_spec(2),
+            row_spec,
+        ],
+        [
+            item_out(lat_rows, BF16),
+            item_out(keys_here, BF16),
+            item_out(keys_here, BF16),
+            (own_spec(video_here), video_tokens.shape, F32),
+            item_out(video_here, BF16),
+            item_out(cap_rows, BF16),
+            (pl.BlockSpec((8, D), lambda i, s: (0, 0)), (8, D), F32),
+        ],
+        (
+            queries, keys, values, lse, attended, d_att, video_tokens, video_other, cap, mask,
+            weights, weights, gain_tok_row,
+        ),
+    )
+    other_here = swap_cores(other_back)
+    (video_grad,) = call(
+        place_kernel,
+        "place_rows",
+        [pl.BlockSpec(memory_space=pl.ANY), item_spec(video_here)],
+        [
+            (
+                pl.BlockSpec((None, video_here, D), lambda i, s: ((1 - s[0]) * own + i, 0, 0)),
+                video_tokens.shape,
+                F32,
+            )
+        ],
+        (video_grad, other_here),
+        aliases={1: 0},
+    )
+    caption_grad = jnp.zeros((txt_count, own, cap_here, D), F32)
+    for step in range(txt_count):
+        perm = [(b, a) for a, b in caption_perm(step, 2, txt_count, 2)]
+        part = lax.ppermute(
+            cap_back[:, step * cap_here : (step + 1) * cap_here], ("vid", "txt"), perm
+        )
+        caption_grad = lax.dynamic_update_index_in_dim(
+            caption_grad, part.astype(F32), (place + step) % txt_count, 0
+        )
+    caption_grad = caption_grad.reshape(caption_tokens.shape)
+
+    d_lat_norm = dot("ble,ed->bld", d_queries, w_query)
+    d_lat_back, gain_lat_part = norm_back_rows(lat.astype(F32), gain_latent, d_lat_norm)
+    lat_grad_mine = d_after + d_lat_back
+
+    def mine_cols(array):
+        return lax.dynamic_slice_in_dim(array, z * head_width, head_width, array.ndim - 1)
+
+    grad_out = dot("ble,bld->ed", mine_cols(mixed_in), d_branch)
+    grad_query = dot("bld,ble->de", lat_norm, mine_cols(d_queries))
+    grad_key = dot("bld,ble->de", tok_norm, mine_cols(d_keys))
+    grad_value = dot("bld,ble->de", tok_norm, mine_cols(d_values))
+    extra = jnp.zeros((8, D), F32)
+    extra = extra.at[0].set(jnp.sum(gain_mlp_part, axis=0)).at[1].set(jnp.sum(keep))
+    grad_up, grad_down, out_rows = lax.psum(
+        (grad_up, grad_down, jnp.concatenate([grad_out, extra])), ("vid", "txt")
+    )
+    gains = jnp.stack([jnp.sum(gain_lat_part, axis=0), gain_tok_part[0]])
+    gains = gains.reshape(2 * D // head_width, head_width)
+    late = jnp.concatenate([grad_query, grad_key, grad_value, gains])
+    late = lax.psum(late.astype(BF16), ("vid", "txt")).astype(F32)
+    gains = late[3 * D :].reshape(2, D)
+
+    def give_back(values):
+        other = swap_cores(values[:, lat_half:].astype(BF16)).astype(values.dtype)
+        whole = jnp.zeros((items_here, lat_half, D), values.dtype)
+        whole = lax.dynamic_update_slice_in_dim(whole, values[:, :lat_half], core * own, 0)
+        return lax.dynamic_update_slice_in_dim(whole, other, (1 - core) * own, 0)
+
+    latents_out = give_back(out_mine)
+    latent_grad = give_back(lat_grad_mine)
+    kept_count = out_rows[head_width + 1, 0].astype(jnp.int32)
+    return (
+        latents_out,
+        latent_grad,
+        video_grad,
+        caption_grad,
+        late[:D],
+        late[D : 2 * D],
+        late[2 * D : 3 * D],
+        out_rows[:head_width],
+        grad_up,
+        grad_down,
+        gains[0],
+        gains[1],
+        out_rows[head_width],
+        kept_count,
+    )
+
+
+def norm_back_rows(values, gain, upstream):
+    mean = jnp.mean(values, axis=-1, keepdims=True)
+    center = values - mean
+    rate = lax.rsqrt(jnp.mean(center * center, axis=-1, keepdims=True) + 1e-05)
+    hat = center * rate
+    scaled = upstream * gain
+    first = jnp.mean(scaled, axis=-1, keepdims=True)
+    second = jnp.mean(scaled * hat, axis=-1, keepdims=True)
+    return rate * (scaled - first - hat * second), jnp.sum(upstream * hat, axis=-2)
+
+
+def fits(mesh):
+    shape = mesh.shape
+    return shape["vid"] == 2 and shape["txt"] == 4 and shape["head"] == 4
+
+
 def solution(mesh):
     in_specs = (
         P("txt", "vid", None),
@@ -421,4 +918,4 @@
         P(),
         P(),
     )
-    return jax.shard_map(local, mesh=mesh, in_specs=in_specs, out_specs=out_specs, check_vma=False)
+    return jax.shard_map(local if fits(mesh) else local_general, mesh=mesh, in_specs=in_specs, out_specs=out_specs, check_vma=False)

time: 1160 us -> 509 us (0.44)
  waiting for transfers between devices: 830 us -> 228 us
  Pallas kernels: 0 us -> 120 us
  blocking collectives: 105 us -> 0 us
  other arithmetic: 71.9 us -> 23.2 us
  matrix products: 73.1 us -> 38.7 us
  starting transfers between devices: 1.28 us -> 33.5 us
    psum x5 -> x3, waiting for transfers between devices: 711 us -> 159 us  [the longest x1 92.5 us: local(): lax.psum((grad_up, grad_down, jnp.concatenate([grad_out, extra])), ('vid'...]
    pallas_call x0 -> x4, Pallas kernels: none -> 120 us  [call(): pl.pallas_call(kernel, name=name, grid_spec=pltpu.PrefetchScalarGridSpec(...]
    reduce_scatter x2 -> x0, waiting for transfers between devices: 83.8 us -> none  [the longest x1 51.8 us: local(): lax.psum_scatter(to_blocks(value_all, vid_count, txt_count), ('vid', 'txt...]
    ppermute x0 -> x23, waiting for transfers between devices: none -> 68.1 us  [the longest x9 65.7 us: head_shift(): lax.ppermute(values, 'head', [(i, (i - shift) % count) for i in range(cou...]
    psum x2 -> x0, blocking collectives: 56.1 us -> none  [the longest x1 28.1 us: local(): lax.psum((grad_query, grad_key, grad_value, grad_out, grad_up, grad_down,...]
    all_gather x2 -> x0, blocking collectives: 48.7 us -> none  [combined_all(): gathered = jax.tree.map(lambda a: lax.all_gather(a, axis), part)]
    reduce_sum x19 -> x6, other arithmetic: 42.4 us -> 3.68 us  [the longest x1 1.37 us: local(): jnp.sum(gain_mlp_part, axis=0)]
    all_gather x2 -> x0, waiting for transfers between devices: 35.6 us -> none  [the longest x1 26.6 us: local(): lax.all_gather(d_att[None], ('vid', 'txt'), axis=0, tiled=True)]
  transfers between devices with their start and end apart: 9 -> 26, of which waited for: 9 -> 10; matrix products, arithmetic and copies ran while one was open for 8% -> 12% of each run, Pallas kernels for 0% -> 0%
where the time goes in v1:
time: 509 us; the launch traced here: 507 us
  waiting for transfers between devices  228 us (45%)
  Pallas kernels  120 us (24%)
  local copies, waits for them, and re-layouts  47.9 us (9%)
  matrix products  38.7 us (8%)
  starting transfers between devices  33.5 us (7%)
  other arithmetic  23.2 us (5%)
  between operations  16.4 us (3%)
    pallas_call x4, Pallas kernels, call(): pl.pallas_call(kernel, name=name, grid_spec=pltpu.PrefetchScalarGridSpec(...  120 us
    psum x1, waiting for transfers between devices, local(): lax.psum((grad_up, grad_down, jnp.concatenate([grad_out, extra])), ('vid'...  92.5 us
    ppermute x9, waiting for transfers between devices, head_shift(): lax.ppermute(values, 'head', [(i, (i - shift) % count) for i in range(cou...  65.7 us
    dot_general x12, matrix products, dot(): return jnp.einsum(spec, a, b, preferred_element_type=F32)  38.7 us
    psum x1, waiting for transfers between devices, local(): late = lax.psum(late.astype(BF16), ('vid', 'txt')).astype(F32)  34.5 us
    psum x1, waiting for transfers between devices, local(): lax.psum(dot('blf,fd->bld', activ, down_weight).astype(BF16), 'head')  32.5 us
    ppermute x9, starting transfers between devices, head_shift(): lax.ppermute(values, 'head', [(i, (i - shift) % count) for i in range(cou...  13.1 us
  transfers between devices with their start and end apart: 26, of which 10 were waited for; matrix products, arithmetic and copies ran while one was open for 12% of the time, Pallas kernels for 0%

profile of v1, /device:TPU:0, one launch (start us, length us, event | category | flops | bytes accessed | tf_op | source)
XLA Modules:
  0.0 507.2 jit_solution(12511748049034078541)
XLA Ops:
  10.3 5.1 %collective-permute-start.6 = (bf16[2,192,768]{2,1,0:T(8,128)(2,1)}, bf16[2,192,768]{2,1,0:T(8,128)(2,1)}, u32[]{:S(2)}, u32[]{:S(2)}) collective-permute-start(bf16[2,192,768]{2,1,0:T(8,128)(2,1)} %get-tuple-element.102), channel_id=1, source_target_pairs={{0,3},{1,0},{2,1},{3,2},{4,7},{5,4},{6,5},{7,6},{8,11},{9,8},{10,9... | collective-permute-start | bytes 1769480 | tf_op jit(solution)/shard_map/ppermute | solution.py:396
  20.8 3.8 constant_dynamic-slice_fusion.3
  24.7 4.7 collective-permute-done.6
  31.5 34.6 %collective-permute-done.7 = bf16[2,192,768]{2,1,0:T(8,128)(2,1)} collective-permute-done((bf16[2,192,768]{2,1,0:T(8,128)(2,1)}, bf16[2,192,768]{2,1,0:T(8,128)(2,1)}, u32[]{:S(2)}, u32[]{:S(2)}) %collective-permute-start.7) | collective-permute-done | bytes 589856 | tf_op jit(solution)/shard_map/ppermute | solution.py:396
  75.4 4.8 collective-permute-start.2
  97.8 9.2 %token_norm.1.tok_ref = bf16[4,1088,768]{2,1,0:T(8,128)(2,1)} custom-call(s32[5]{0:T(128)} %pad_add_fusion.s_ref, bf16[8,512,768]{2,1,0:T(8,128)(2,1)} %own_ref.3, bf16[4,512,768]{2,1,0:T(8,128)(2,1)} %collective-permute-done.other_ref, bf16[4,64,768]{2,1,0:T(8,128)(2,1)} %pad_maximum_fusion.4.cap_ref, f32[1,768]{1,0:T(1,128)} %broadcast_in_dim.112.gain_ref), custom_call_target="tpu_custom_call" | custom-call | tf_op jit(solution)/shard_map/token_norm/pallas_call | solution.py:697
  107.8 46.4 %attention_forward.1 = (bf16[4,128,768]{2,1,0:T(8,128)(2,1)}, bf16[4,128,768]{2,1,0:T(8,128)(2,1)}, bf16[4,1088,768]{2,1,0:T(8,128)(2,1)}, bf16[4,1088,768]{2,1,...) custom-call(s32[5]{0:T(128)} %pad_add_fusion.s_ref, ...), custom_call_target="tpu_custom_call" | custom-call | tf_op jit(solution)/shard_map/attention_forward/pallas_call | solution.py:697
  154.3 6.2 %multiply_convert_fusion.1 = (bf16[4,128,768]{2,1,0:T(8,128)(2,1)}, f32[4,128,768]{2,1,0:T(8,128)S(1)}, f32[4,128,768]{2,1,0:T(8,128)S(1)}) fusion(bf16[4,128,768]{2,1,0:T(8,128)(2,1)} %get-tuple-element.69, bf16[768,768]{1,0:T(8,128)(2,1)S(1)} %copy-done), kind=kOutput, calls=%fused_computation.37 | convolution fusion | flops 629538816 | bytes 5898240 | tf_op jit(solution)/shard_map/bld,df->blf/dot_general | solution.py:642
  167.5 3.3 convolution_bitcast_fusion.1
  171.6 10.8 %collective-permute-done.11 = bf16[128,768]{1,0:T(8,128)(2,1)} collective-permute-done((bf16[128,768]{1,0:T(8,128)(2,1)}, bf16[128,768]{1,0:T(8,128)(2,1)}, u32[]{:S(2)}, u32[]{:S(2)}) %collective-permute-start.11) | collective-permute-done | bytes 196640 | tf_op jit(solution)/shard_map/ppermute | solution.py:396
  189.5 14.1 %collective-permute-done.14 = bf16[128,768]{1,0:T(8,128)(2,1)S(1)} collective-permute-done((bf16[128,768]{1,0:T(8,128)(2,1)S(1)}, bf16[128,768]{1,0:T(8,128)(2,1)S(1)}, u32[]{:S(2)}, u32[]{:S(2)}) %collective-permute-start.14) | collective-permute-done | bytes 196640 | tf_op jit(solution)/shard_map/ppermute | solution.py:396
  211.9 3.5 convolution_bitcast_fusion
  215.4 32.5 %all-reduce.7.cloned.1.call-done = bf16[4,128,768]{2,1,0:T(8,128)(2,1)} async-done(((bf16[4,128,768]{2,1,0:T(8,128)(2,1)}), bf16[4,128,768]{2,1,0:T(8,128)(2,1)}) %all-reduce.7.cloned.1.call-update) | async-done | bytes 786448 | tf_op jit(solution)/shard_map/psum | solution.py:752
  247.8 2.9 fusion.20
  252.5 58.4 %attention_backward.1 = (bf16[4,128,768]{2,1,0:T(8,128)(2,1)}, bf16[4,1088,768]{2,1,0:T(8,128)(2,1)}, bf16[4,1088,768]{2,1,0:T(8,128)(2,1)}, f32[8,512,768]{2,1,...) custom-call(s32[5]{0:T(128)} %pad_add_fusion.s_ref, ...), custom_call_target="tpu_custom_call" | custom-call | tf_op jit(solution)/shard_map/attention_backward/pallas_call | solution.py:697
  310.9 3.9 fusion.16
  317.3 6.2 %fusion.36 = bf16[768,192]{0,1:T(8,128)(2,1)S(1)} fusion(bf16[4,1088,768]{2,1,0:T(8,128)(2,1)} %token_norm.1.tok_ref, bf16[4,1088,768]{2,1,0:T(8,128)(2,1)} %get-tuple-element.83, s32[]{:T(128)S(6)} %select_n.170), kind=kOutput, calls=%fused_computation.59 | convolution fusion | flops 1283604480 | bytes 9207812 | tf_op jit(solution)/shard_map/bld,ble->de/dot_general | solution.py:642
  323.4 6.2 %fusion.39 = bf16[768,192]{0,1:T(8,128)(2,1)S(1)} fusion(bf16[4,1088,768]{2,1,0:T(8,128)(2,1)} %token_norm.1.tok_ref, bf16[4,1088,768]{2,1,0:T(8,128)(2,1)} %get-tuple-element.82, s32[]{:T(128)S(6)} %select_n.170), kind=kOutput, calls=%fused_computation.60 | convolution fusion | flops 1283604480 | bytes 9207812 | tf_op jit(solution)/shard_map/bld,ble->de/dot_general | solution.py:642
  333.6 4.1 collective-permute-start.20
  337.8 3.9 collective-permute-start.22
  352.8 34.5 %all-reduce.9.cloned.1.call-done = bf16[2312,192]{0,1:T(8,128)(2,1)} async-done(((bf16[2312,192]{0,1:T(8,128)(2,1)}), bf16[2312,192]{0,1:T(8,128)(2,1)}) %all-reduce.9.cloned.1.call-update) | async-done | bytes 887824 | tf_op jit(solution)/shard_map/psum | solution.py:840
  389.8 2.4 fusion.74
  392.2 92.5 %all-reduce.11.cloned.1.call-done = (f32[200,768]{1,0:T(8,128)}, f32[768,768]{1,0:T(8,128)}, f32[768,768]{1,0:T(8,128)}) async-done(((f32[200,768]{1,0:T(8,128)}, f32[768,768]{1,0:T(8,128)}, f32[768,768]{1,0:T(8,128)}), (f32[200,768]{1,0:T(8,128)}, f32[768,768]{1,0:T(8,128)}, f32[768,768]{1,0:T(8,128)})) %all-reduce.11.cloned.1.call-update) | async-done | bytes 5333008 | tf_op jit(solution)/shard_map/psum | solution.py:834
  489.8 5.8 %place_rows.1 = f32[8,512,768]{2,1,0:T(8,128)} custom-call(s32[5]{0:T(128)} %pad_add_fusion.s_ref, f32[8,512,768]{2,1,0:T(8,128)} %get-tuple-element.78.whole_ref, bf16[4,512,768]{2,1,0:T(8,128)(2,1)} %collective-permute-done.18.part_ref), custom_call_target="tpu_custom_call", output_to_operand_aliasing={{}: (1, {})} | custom-call | tf_op jit(solution)/shard_map/place_rows/pallas_call | solution.py:697
  (230 shorter events, 91.1 us)
Async XLA Ops:
  7.2 240.6 %all-reduce.7.cloned.1.call-start = ((), (), s32[]{:S(2)}) async-start(), calls=%async_computation | async-start | bytes 1572864 | tf_op jit(solution)/shard_map/psum | solution.py:752
  10.3 19.2 %collective-permute-start.6 = (bf16[2,192,768]{2,1,0:T(8,128)(2,1)}, bf16[2,192,768]{2,1,0:T(8,128)(2,1)}, u32[]{:S(2)}, u32[]{:S(2)}) collective-permute-start(bf16[2,192,768]{2,1,0:T(8,128)(2,1)} %get-tuple-element.102), channel_id=1, source_target_pairs={{0,3},{1,0},{2,1},{3,2},{4,7},{5,4},{6,5},{7,6},{8,11},{9,8},{10,9... | collective-permute-start | bytes 1769480 | tf_op jit(solution)/shard_map/ppermute | solution.py:396
  15.4 50.7 %collective-permute-start.7 = (bf16[2,192,768]{2,1,0:T(8,128)(2,1)}, bf16[2,192,768]{2,1,0:T(8,128)(2,1)}, u32[]{:S(2)}, u32[]{:S(2)}) collective-permute-start(bf16[2,192,768]{2,1,0:T(8,128)(2,1)} %get-tuple-element.102), channel_id=1, source_target_pairs={{0,2},{1,3},{2,0},{3,1},{4,6},{5,7},{6,4},{7,5},{8,10},{9,11},{10,... | collective-permute-start | bytes 1769480 | tf_op jit(solution)/shard_map/ppermute | solution.py:396
  15.4 52.6 %collective-permute-start.8 = (bf16[2,192,768]{2,1,0:T(8,128)(2,1)}, bf16[2,192,768]{2,1,0:T(8,128)(2,1)}, u32[]{:S(2)}, u32[]{:S(2)}) collective-permute-start(bf16[2,192,768]{2,1,0:T(8,128)(2,1)} %get-tuple-element.102), channel_id=1, source_target_pairs={{0,1},{1,2},{2,3},{3,0},{4,5},{5,6},{6,7},{7,4},{8,9},{9,10},{10,1... | collective-permute-start | bytes 1769480 | tf_op jit(solution)/shard_map/ppermute | solution.py:396
  17.4 57.3 %collective-permute-start.3 = (bf16[4,17,768]{2,1,0:T(8,128)(2,1)}, bf16[4,17,768]{2,1,0:T(8,128)(2,1)}, u32[]{:S(2)}, u32[]{:S(2)}) collective-permute-start(bf16[4,17,768]{2,1,0:T(8,128)(2,1)} %get-tuple-element.123), channel_id=1, source_target_pairs={{0,4},{4,20},{8,0},{12,16},{16,12},{20,28},{24,8},{28,24},{1,5},{5... | collective-permute-start | bytes 313352 | tf_op jit(solution)/shard_map/ppermute | solution.py:675
  18.9 56.5 %collective-permute-start.4 = (bf16[4,17,768]{2,1,0:T(8,128)(2,1)}, bf16[4,17,768]{2,1,0:T(8,128)(2,1)}, u32[]{:S(2)}, u32[]{:S(2)}) collective-permute-start(bf16[4,17,768]{2,1,0:T(8,128)(2,1)} %get-tuple-element.124), channel_id=1, source_target_pairs={{0,20},{4,0},{8,16},{12,4},{16,28},{20,8},{24,24},{28,12},{1,21},{... | collective-permute-start | bytes 313352 | tf_op jit(solution)/shard_map/ppermute | solution.py:675
  29.5 68.4 %collective-permute-start = (bf16[4,512,768]{2,1,0:T(8,128)(2,1)}, bf16[4,512,768]{2,1,0:T(8,128)(2,1)}, u32[]{:S(2)}, u32[]{:S(2)}) collective-permute-start(bf16[4,512,768]{2,1,0:T(8,128)(2,1)} %constant_dynamic-slice_fusion.3), channel_id=1, source_target_pairs={{0,16},{16,0},{1,17},{17,1},{2,18},{18,2},{3,19},{19,3},{4,20},{20... | collective-permute-start | bytes 9437192 | tf_op jit(solution)/shard_map/ppermute | solution.py:392
  70.0 23.0 %collective-permute-start.9 = (bf16[4,2,192,768]{3,2,1,0:T(8,128)(2,1)}, bf16[4,2,192,768]{3,2,1,0:T(8,128)(2,1)}, u32[]{:S(2)}, u32[]{:S(2)}) collective-permute-start(bf16[4,2,192,768]{3,2,1,0:T(8,128)(2,1)} %bitcast_dynamic-update-slice_fusion.2), channel_id=1, source_target_pairs={{0,16},{16,0},{1,17},{17,1},{2,18},{18,2},{3,19},{19,3},{4,20},{20... | collective-permute-start | bytes 7077896 | tf_op jit(solution)/shard_map/ppermute | solution.py:392
  71.1 18.6 %collective-permute-start.5 = (bf16[4,128,768]{2,1,0:T(8,128)(2,1)}, bf16[4,128,768]{2,1,0:T(8,128)(2,1)}, u32[]{:S(2)}, u32[]{:S(2)}) collective-permute-start(bf16[4,128,768]{2,1,0:T(8,128)(2,1)} %constant_dynamic-slice_fusion), channel_id=1, source_target_pairs={{0,16},{16,0},{1,17},{17,1},{2,18},{18,2},{3,19},{19,3},{4,20},{20... | collective-permute-start | bytes 2359304 | tf_op jit(solution)/shard_map/ppermute | solution.py:392
  74.7 9.9 %collective-permute-start.1 = (bf16[4,17,768]{2,1,0:T(8,128)(2,1)S(1)}, bf16[4,17,768]{2,1,0:T(8,128)(2,1)S(1)}, u32[]{:S(2)}, u32[]{:S(2)}) collective-permute-start(bf16[4,17,768]{2,1,0:T(8,128)(2,1)S(1)} %get-tuple-element.121), channel_id=1, source_target_pairs={{0,0},{4,16},{8,4},{12,20},{16,8},{20,24},{24,12},{28,28},{1,1},{5... | collective-permute-start | bytes 313352 | tf_op jit(solution)/shard_map/ppermute | solution.py:675
  75.4 9.2 %collective-permute-start.2 = (bf16[4,17,768]{2,1,0:T(8,128)(2,1)S(1)}, bf16[4,17,768]{2,1,0:T(8,128)(2,1)S(1)}, u32[]{:S(2)}, u32[]{:S(2)}) collective-permute-start(bf16[4,17,768]{2,1,0:T(8,128)(2,1)S(1)} %get-tuple-element.122), channel_id=1, source_target_pairs={{0,16},{4,4},{8,20},{12,0},{16,24},{20,12},{24,28},{28,8},{1,17},{... | collective-permute-start | bytes 313352 | tf_op jit(solution)/shard_map/ppermute | solution.py:675
  164.4 7.2 %collective-permute-start.10 = (bf16[128,768]{1,0:T(8,128)(2,1)}, bf16[128,768]{1,0:T(8,128)(2,1)S(1)}, u32[]{:S(2)}, u32[]{:S(2)}) collective-permute-start(bf16[128,768]{1,0:T(8,128)(2,1)} %get-tuple-element.116), channel_id=1, source_target_pairs={{0,3},{1,0},{2,1},{3,2},{4,7},{5,4},{6,5},{7,6},{8,11},{9,8},{10,9... | collective-permute-start | bytes 589832 | tf_op jit(solution)/shard_map/ppermute | solution.py:396
  164.4 18.0 %collective-permute-start.11 = (bf16[128,768]{1,0:T(8,128)(2,1)}, bf16[128,768]{1,0:T(8,128)(2,1)}, u32[]{:S(2)}, u32[]{:S(2)}) collective-permute-start(bf16[128,768]{1,0:T(8,128)(2,1)} %get-tuple-element.118), channel_id=1, source_target_pairs={{0,2},{1,3},{2,0},{3,1},{4,6},{5,7},{6,4},{7,5},{8,10},{9,11},{10,... | collective-permute-start | bytes 589832 | tf_op jit(solution)/shard_map/ppermute | solution.py:396
  165.3 17.1 %collective-permute-start.12 = (bf16[128,768]{1,0:T(8,128)(2,1)S(1)}, bf16[128,768]{1,0:T(8,128)(2,1)}, u32[]{:S(2)}, u32[]{:S(2)}) collective-permute-start(bf16[128,768]{1,0:T(8,128)(2,1)S(1)} %get-tuple-element.117), channel_id=1, source_target_pairs={{0,1},{1,2},{2,3},{3,0},{4,5},{5,6},{6,7},{7,4},{8,9},{9,10},{10,1... | collective-permute-start | bytes 589832 | tf_op jit(solution)/shard_map/ppermute | solution.py:396
  183.7 5.7 %collective-permute-start.13 = (bf16[128,768]{1,0:T(8,128)(2,1)S(1)}, bf16[128,768]{1,0:T(8,128)(2,1)S(1)}, u32[]{:S(2)}, u32[]{:S(2)}) collective-permute-start(bf16[128,768]{1,0:T(8,128)(2,1)S(1)} %get-tuple-element.98), channel_id=1, source_target_pairs={{0,3},{1,0},{2,1},{3,2},{4,7},{5,4},{6,5},{7,6},{8,11},{9,8},{10,9... | collective-permute-start | bytes 589832 | tf_op jit(solution)/shard_map/ppermute | solution.py:396
  184.7 18.9 %collective-permute-start.14 = (bf16[128,768]{1,0:T(8,128)(2,1)S(1)}, bf16[128,768]{1,0:T(8,128)(2,1)S(1)}, u32[]{:S(2)}, u32[]{:S(2)}) collective-permute-start(bf16[128,768]{1,0:T(8,128)(2,1)S(1)} %get-tuple-element.98), channel_id=1, source_target_pairs={{0,2},{1,3},{2,0},{3,1},{4,6},{5,7},{6,4},{7,5},{8,10},{9,11},{10,... | collective-permute-start | bytes 589832 | tf_op jit(solution)/shard_map/ppermute | solution.py:396
  186.7 16.8 %collective-permute-start.15 = (bf16[128,768]{1,0:T(8,128)(2,1)S(1)}, bf16[128,768]{1,0:T(8,128)(2,1)S(1)}, u32[]{:S(2)}, u32[]{:S(2)}) collective-permute-start(bf16[128,768]{1,0:T(8,128)(2,1)S(1)} %get-tuple-element.98), channel_id=1, source_target_pairs={{0,1},{1,2},{2,3},{3,0},{4,5},{5,6},{6,7},{7,4},{8,9},{9,10},{10,1... | collective-permute-start | bytes 589832 | tf_op jit(solution)/shard_map/ppermute | solution.py:396
  205.3 182.0 %all-reduce.9.cloned.1.call-start = ((), (), s32[]{:S(2)}) async-start(), calls=%async_computation.1 | async-start | bytes 1867776 | tf_op jit(solution)/shard_map/psum | solution.py:840
  330.6 154.0 %all-reduce.11.cloned.1.call-start = ((), (), s32[]{:S(2)}) async-start(), calls=%async_computation.2 | async-start | bytes 10665984 | tf_op jit(solution)/shard_map/psum | solution.py:834
  331.5 16.7 %collective-permute-start.19 = (bf16[4,16,768]{2,1,0:T(8,128)(2,1)}, bf16[4,16,768]{2,1,0:T(8,128)(2,1)}, u32[]{:S(2)}, u32[]{:S(2)}) collective-permute-start(bf16[4,16,768]{2,1,0:T(8,128)(2,1)} %get-tuple-element.128), channel_id=1, source_target_pairs={{0,0},{16,4},{4,8},{20,12},{8,16},{24,20},{12,24},{28,28},{1,1},{1... | collective-permute-start | bytes 294920 | tf_op jit(solution)/shard_map/ppermute | solution.py:813
  333.6 16.1 %collective-permute-start.20 = (bf16[4,16,768]{2,1,0:T(8,128)(2,1)}, bf16[4,16,768]{2,1,0:T(8,128)(2,1)}, u32[]{:S(2)}, u32[]{:S(2)}) collective-permute-start(bf16[4,16,768]{2,1,0:T(8,128)(2,1)} %get-tuple-element.127), channel_id=1, source_target_pairs={{16,0},{4,4},{20,8},{0,12},{24,16},{12,20},{28,24},{8,28},{17,1},{... | collective-permute-start | bytes 294920 | tf_op jit(solution)/shard_map/ppermute | solution.py:813
  337.7 13.1 %collective-permute-start.21 = (bf16[4,16,768]{2,1,0:T(8,128)(2,1)}, bf16[4,16,768]{2,1,0:T(8,128)(2,1)}, u32[]{:S(2)}, u32[]{:S(2)}) collective-permute-start(bf16[4,16,768]{2,1,0:T(8,128)(2,1)} %get-tuple-element.126), channel_id=1, source_target_pairs={{4,0},{20,4},{0,8},{16,12},{12,16},{28,20},{8,24},{24,28},{5,1},{2... | collective-permute-start | bytes 294920 | tf_op jit(solution)/shard_map/ppermute | solution.py:813
  337.8 13.9 %collective-permute-start.22 = (bf16[4,16,768]{2,1,0:T(8,128)(2,1)}, bf16[4,16,768]{2,1,0:T(8,128)(2,1)}, u32[]{:S(2)}, u32[]{:S(2)}) collective-permute-start(bf16[4,16,768]{2,1,0:T(8,128)(2,1)} %get-tuple-element.125), channel_id=1, source_target_pairs={{20,0},{0,4},{16,8},{4,12},{28,16},{8,20},{24,24},{12,28},{21,1},{... | collective-permute-start | bytes 294920 | tf_op jit(solution)/shard_map/ppermute | solution.py:813
  341.7 148.1 %collective-permute-start.18 = (bf16[4,512,768]{2,1,0:T(8,128)(2,1)}, bf16[4,512,768]{2,1,0:T(8,128)(2,1)}, u32[]{:S(2)}, u32[]{:S(2)}) collective-permute-start(bf16[4,512,768]{2,1,0:T(8,128)(2,1)} %get-tuple-element.79), channel_id=1, source_target_pairs={{0,16},{16,0},{1,17},{17,1},{2,18},{18,2},{3,19},{19,3},{4,20},{20... | collective-permute-start | bytes 9437192 | tf_op jit(solution)/shard_map/ppermute | solution.py:392
  (45 other events, 807.2 us)
Sparse Core Ops, SparseCore 0:
  205.4 42.3 all-reduce.6
  330.8 56.4 all-reduce.8
  391.5 93.1 all-reduce.10

commit v2 on v1

--- a/solution.py
+++ b/solution.py
@@ -415,6 +415,29 @@
     return result
 
 
+def sum_over_group(rows, core, place, count):
+    half = rows.shape[0] // 2
+    part = half // count
+    total = take_block(rows, core, half)
+    total = total + swap_cores(take_block(rows, 1 - core, half).astype(BF16)).astype(F32)
+    low = total.astype(BF16)
+    total = take_block(total, place, part)
+    for step in range(1, count):
+        perm = [(i, (i - step) % count) for i in range(count)]
+        chunk = take_block(low, (place - step) % count, part)
+        total = total + lax.ppermute(chunk, "txt", perm).astype(F32)
+    total = total.astype(BF16)
+    mine = lax.dynamic_update_slice_in_dim(jnp.zeros_like(low), total, place * part, 0)
+    for step in range(1, count):
+        perm = [(i, (i - step) % count) for i in range(count)]
+        mine = lax.dynamic_update_slice_in_dim(
+            mine, lax.ppermute(total, "txt", perm), (place + step) % count * part, 0
+        )
+    whole = jnp.zeros(rows.shape, BF16)
+    whole = lax.dynamic_update_slice_in_dim(whole, mine, core * half, 0)
+    return lax.dynamic_update_slice_in_dim(whole, swap_cores(mine), (1 - core) * half, 0)
+
+
 def caption_perm(step, vid_count, txt_count, cores):
     pairs = []
     for v in range(vid_count):
@@ -463,8 +486,9 @@
     return [(start, size) for start in range(0, video, size)] + [(video, cap)]
 
 
-def norm_kernel(s_ref, own_ref, other_ref, cap_ref, gain_ref, out_ref):
+def norm_kernel(s_ref, own_ref, other_ref, cap_ref, lat_ref, gain_ref, gain_lat_ref, out_ref, lat_out):
     gain = gain_ref[...]
+    lat_out[...] = layer_norm(lat_ref[...].astype(F32), gain_lat_ref[...]).astype(BF16)
     start = 0
     for ref in (own_ref, other_ref, cap_ref):
         rows = ref.shape[0]
@@ -475,23 +499,21 @@
         start += rows
 
 
-def forward_kernel(
-    s_ref, tok_ref, lat_ref, mask_ref, wq_ref, wk_ref, wv_ref, wo_ref, gain_lat_ref, gain_mlp_ref,
-    q_ref, latn_ref, k_ref, v_ref, lse_ref, o_ref, mix_ref, after_ref, mlpn_ref, s_scr,
-):
-    item = pl.program_id(0)
-    lat = lat_ref[...].astype(F32)
-    latn = layer_norm(lat, gain_lat_ref[...]).astype(BF16)
-    latn_ref[...] = latn
-    q_ref[...] = (dot_nt(latn, square(wq_ref)).astype(BF16).astype(F32) * 0.125).astype(BF16)
-    keys = tok_ref.shape[0]
+def forward_kernel(s_ref, tok_ref, latn_ref, mask_ref, wq_ref, wk_ref, wv_ref, *refs):
+    q_ref, k_ref, v_ref, lse_ref, o_ref, s_scr = refs[-6:]
+    keys, width = k_ref.shape
     cap = mask_ref.shape[0]
     step = keys // 4
 
+    def matrix(ref):
+        return ref[...].reshape(width, D)
+
+    q_ref[...] = (dot_nt(latn_ref[...], matrix(wq_ref)).astype(BF16).astype(F32) * 0.125).astype(BF16)
+
     def project(c, carry):
         rows = pl.ds(pl.multiple_of(c * step, 16), step)
-        k_ref[rows, :] = dot_nt(tok_ref[rows, :], square(wk_ref)).astype(BF16)
-        v_ref[rows, :] = dot_nt(tok_ref[rows, :], square(wv_ref)).astype(BF16)
+        k_ref[rows, :] = dot_nt(tok_ref[rows, :], matrix(wk_ref)).astype(BF16)
+        v_ref[rows, :] = dot_nt(tok_ref[rows, :], matrix(wv_ref)).astype(BF16)
         return carry
 
     lax.fori_loop(0, 4, project, 0)
@@ -521,19 +543,13 @@
         lse_ref[pl.ds(p, 1), :] = peak + jnp.log(total)
         return carry
 
-    lax.fori_loop(0, D // PAIR, pair, 0)
-    keep = (1 - s_ref[1 + item]).astype(F32)
-    mixed = (o_ref[...] * keep).astype(BF16)
-    mix_ref[...] = mixed
-    after = lat + dot_nn(mixed, square(wo_ref))
-    after_ref[...] = after
-    mlpn_ref[...] = layer_norm(after, gain_mlp_ref[...]).astype(BF16)
+    lax.fori_loop(0, width // PAIR, pair, 0)
 
 
 def backward_kernel(
     s_ref, q_ref, k_ref, v_ref, lse_ref, o_ref, datt_ref, own_ref, other_ref, cap_ref, mask_ref,
-    wk_ref, wv_ref, gain_ref,
-    dq_ref, dk_ref, dv_ref, own_out, other_out, cap_out, gain_out,
+    wk_ref, wv_ref, gain_ref, tok_ref,
+    dq_ref, gk_ref, gv_ref, own_out, other_out, cap_out, gain_out, dk_ref, dv_ref,
 ):
     item = pl.program_id(0)
     keys = k_ref.shape[0]
@@ -553,7 +569,8 @@
             ],
             axis=1,
         )
-        lse = lse_ref[pl.ds(p, 1), :]
+        pairs_here = D // PAIR // lse_ref.shape[0]
+        lse = lse_ref[p // pairs_here, pl.ds(p % pairs_here, 1), :]
         dq = jnp.zeros((PAIR, q2.shape[0]), F32)
         for start, size in chunks:
             rows = pl.ds(start, size)
@@ -577,6 +594,12 @@
     @pl.when(item == 0)
     def _():
         gain_out[...] = jnp.zeros_like(gain_out)
+        gk_ref[...] = jnp.zeros_like(gk_ref)
+        gv_ref[...] = jnp.zeros_like(gv_ref)
+
+    window = pl.ds(pl.multiple_of(s_ref[2], PAIR), gk_ref.shape[0])
+    gk_ref[...] += dot_tn(dk_ref[:, window], tok_ref[...])
+    gv_ref[...] += dot_tn(dv_ref[:, window], tok_ref[...])
 
     start = 0
     for ref, out, size in ((own_ref, own_out, 256), (other_ref, other_out, 256), (cap_ref, cap_out, cap)):
@@ -643,15 +666,39 @@
 
     packed = jnp.stack([query_weight.T, key_matrix.T, value_matrix.T, out_weight])
     half = take_block(packed, core, 2)
-    mine = jnp.zeros((head_count,) + half.shape, BF16)
-    mine = lax.dynamic_update_index_in_dim(mine, half, z, 0)
-    for shift in range(1, head_count):
-        mine = lax.dynamic_update_index_in_dim(
-            mine, head_shift(half, shift, head_count), (z + shift) % head_count, 0
-        )
-    weights = jnp.zeros((2,) + mine.shape, BF16)
-    weights = lax.dynamic_update_index_in_dim(weights, mine, core, 0)
-    weights = lax.dynamic_update_index_in_dim(weights, swap_cores(mine), 1 - core, 0)
+    up1 = lax.ppermute(half, "head", [(0, 1), (1, 2), (2, 3)])
+    down1 = lax.ppermute(half, "head", [(1, 0), (2, 1), (3, 2)])
+    partner = jnp.where(z % 2 == 1, up1, down1)
+    near_at = z // 2
+    zero = jnp.int32(0)
+    own_at = z % 2
+    part_shape = (2, 2, 2, head_width, D)
+
+    def place_chunk(whole, chunk, at_core, at_chunk):
+        chunk = chunk.reshape((-1, 1) + chunk.shape[-3:])
+        return lax.dynamic_update_slice(whole, chunk, (at_core, at_chunk, zero, zero, zero))
+
+    near = jnp.zeros(part_shape, BF16)
+    near = place_chunk(near, packed.reshape((2, 2) + packed.shape[1:]), zero, own_at)
+    near = place_chunk(near, partner, core, 1 - own_at)
+    near = place_chunk(near, swap_cores(partner), 1 - core, 1 - own_at)
+    up1, down1, half_then = lax.optimization_barrier((up1, down1, half))
+    up2 = lax.ppermute(up1, "head", [(1, 2), (2, 3)])
+    down2 = lax.ppermute(down1, "head", [(1, 0), (2, 1)])
+    up3 = lax.ppermute(half_then, "head", [(0, 3)])
+    down3 = lax.ppermute(half_then, "head", [(3, 0)])
+
+    def by_place(*choices):
+        low = jnp.where(z == 0, choices[0], choices[1])
+        return jnp.where(z < 2, low, jnp.where(z == 2, choices[2], choices[3]))
+
+    far_mine = jnp.stack([by_place(down2, down1, up2, up3), by_place(down3, down2, up1, up2)])
+    far = jnp.zeros(part_shape, BF16)
+    far = lax.dynamic_update_index_in_dim(far, far_mine, core, 0)
+    far = lax.dynamic_update_index_in_dim(far, swap_cores(far_mine), 1 - core, 0)
+    weights = jnp.zeros((2,) + part_shape, BF16)
+    weights = lax.dynamic_update_index_in_dim(weights, near, near_at, 0)
+    weights = lax.dynamic_update_index_in_dim(weights, far, 1 - near_at, 0)
 
     video_other = swap_cores(take_block(video_tokens, 1 - core, own))
     both = jnp.concatenate([latents, cotangent], axis=1)
@@ -661,7 +708,9 @@
     cot = jnp.concatenate([both_own[:, lat_half:], both_other[:, lat_half:]], axis=1)
     drop_own = take_block(drop_flags, core, own)
     keep = (1 - drop_own).astype(F32)
-    scalars = jnp.concatenate([core[None].astype(jnp.int32), drop_own])
+    window = z * head_width // PAIR * PAIR
+    scalars = jnp.stack([core, near_at, window])
+    scalars_far = jnp.stack([core, 1 - near_at, window])
 
     place_slots = place * cap_here + jnp.arange(cap_here, dtype=jnp.int32)
     cap_valid = (place_slots[None, :] < caption_len[:, None]) & (key_mask == 1)
@@ -686,14 +735,24 @@
 
     def weight_spec(m):
         return pl.BlockSpec(
-            (None, head_count, None, head_width, D),
+            (2, None, 2, None, head_width, D),
+            lambda i, s: (0, m // 2, 0, m % 2, 0, 0),
+            pipeline_mode=pl.Buffered(1),
+        )
+
+    def part_spec(m):
+        return pl.BlockSpec(
+            (None, 2, None, head_width, D),
             lambda i, s: (m // 2, 0, m % 2, 0, 0),
             pipeline_mode=pl.Buffered(1),
         )
 
+    def half_spec(rows):
+        return pl.BlockSpec((None, rows, 2 * head_width), lambda i, s: (i, 0, s[1]))
+
     row_spec = pl.BlockSpec((1, D), lambda i, s: (0, 0))
 
-    def call(kernel, name, ins, outs, operands, scratch=(), aliases={}):
+    def call(kernel, name, ins, outs, operands, micros, scratch=(), aliases={}, scalars=scalars):
         return pl.pallas_call(
             kernel,
             name=name,
@@ -706,6 +765,9 @@
             ),
             out_shape=[jax.ShapeDtypeStruct(shape, dtype) for _, shape, dtype in outs],
             input_output_aliases=aliases,
+            cost_estimate=pl.CostEstimate(
+                flops=micros * 1100 * 10**6, transcendentals=0, bytes_accessed=micros * 10**6
+            ),
             compiler_params=pltpu.CompilerParams(vmem_limit_bytes=56 << 20),
         )(scalars, *operands)
 
@@ -715,33 +777,48 @@
     gain_lat_row = gain_latent[None]
     gain_tok_row = gain_tokens[None]
     gain_mlp_row = gain_mlp[None]
-    (tok_norm,) = call(
+    tok_norm, lat_norm = call(
         norm_kernel,
         "token_norm",
-        [own_spec(video_here), item_spec(video_here), item_spec(cap_rows), row_spec],
-        [item_out(keys_here, BF16)],
-        (video_tokens, video_other, cap, gain_tok_row),
-    )
-    queries, lat_norm, keys, values, lse, attended, mixed_in, after_attn, mlp_norm = call(
-        forward_kernel,
-        "attention_forward",
-        [item_spec(keys_here), item_spec(lat_rows), item_spec(cap_rows, lat_rows)]
-        + [weight_spec(m) for m in range(4)]
+        [own_spec(video_here), item_spec(video_here), item_spec(cap_rows), item_spec(lat_rows)]
         + [row_spec, row_spec],
-        [
-            item_out(lat_rows, BF16),
-            item_out(lat_rows, BF16),
-            item_out(keys_here, BF16),
-            item_out(keys_here, BF16),
-            item_out(8, F32, 2 * lat_rows),
-            item_out(lat_rows, F32),
-            item_out(lat_rows, BF16),
-            item_out(lat_rows, F32),
-            item_out(lat_rows, BF16),
-        ],
-        (tok_norm, lat, mask, weights, weights, weights, weights, gain_lat_row, gain_mlp_row),
-        [pltpu.VMEM((keys_here, 2 * lat_rows), F32)],
-    )
+        [item_out(keys_here, BF16), item_out(lat_rows, BF16)],
+        (video_tokens, video_other, cap, lat, gain_tok_row, gain_lat_row),
+        9,
+    )
+
+    def forward(part, scalars, before=()):
+        return call(
+            forward_kernel,
+            "attention_forward",
+            [item_spec(keys_here), item_spec(lat_rows), item_spec(cap_rows, lat_rows)]
+            + [part_spec(m) for m in range(3)]
+            + [pl.BlockSpec(memory_space=pl.ANY)] * len(before),
+            [
+                (half_spec(lat_rows), (own, lat_rows, D), BF16),
+                (half_spec(keys_here), (own, keys_here, D), BF16),
+                (half_spec(keys_here), (own, keys_here, D), BF16),
+                (
+                    pl.BlockSpec((None, None, 8, 2 * lat_rows), lambda i, s: (i, s[1], 0, 0)),
+                    (own, 2, 8, 2 * lat_rows),
+                    F32,
+                ),
+                (half_spec(lat_rows), (own, lat_rows, D), F32),
+            ],
+            (tok_norm, lat_norm, mask, part, part, part) + tuple(before),
+            23,
+            [pltpu.VMEM((keys_here, 2 * lat_rows), F32)],
+            {7 + n: n for n in range(len(before))},
+            scalars,
+        )
+
+    queries, keys, values, lse, attended = forward(far, scalars_far, forward(near, scalars))
+    w_query = weights[:, 0, :, 0].reshape(D, D)
+    w_out = weights[:, 1, :, 1].reshape(D, D)
+    lat_float = lat.astype(F32)
+    mixed_in = (attended * keep[:, None, None]).astype(BF16)
+    after_attn = lat_float + dot("ble,ed->bld", mixed_in, w_out)
+    mlp_norm = layer_norm(after_attn, gain_mlp).astype(BF16)
 
     pre_act = dot("bld,df->blf", mlp_norm, up_weight)
     activ, gelu_pull = jax.vjp(gelu_exact, pre_act)
@@ -752,22 +829,19 @@
     growth = lax.psum(dot("blf,fd->bld", activ, down_weight).astype(BF16), "head")
     grad_down = dot("blf,bld->fd", activ, cot)
     grad_up = dot("bld,blf->df", mlp_norm, d_pre)
-    out_mine = (after_attn + growth.astype(F32)).astype(BF16)
 
     d_after_norm, gain_mlp_part = norm_back_rows(after_attn, gain_mlp, d_mlp_norm.astype(F32))
     d_after = cot.astype(F32) + d_after_norm
     d_branch = d_after.astype(BF16)
-    w_query = weights[0, :, 0].reshape(D, D)
-    w_out = weights[1, :, 1].reshape(D, D)
     d_att = (dot("bld,ed->ble", d_branch, w_out) * keep[:, None, None]).astype(BF16)
-    d_queries, d_keys, d_values, video_grad, other_back, cap_back, gain_tok_part = call(
+    d_queries, key_rows, value_rows, video_grad, other_back, cap_back, gain_tok_part = call(
         backward_kernel,
         "attention_backward",
         [
             item_spec(lat_rows),
             item_spec(keys_here),
             item_spec(keys_here),
-            item_spec(8, 2 * lat_rows),
+            pl.BlockSpec((None, 2, 8, 2 * lat_rows), lambda i, s: (i, 0, 0, 0)),
             item_spec(lat_rows),
             item_spec(lat_rows),
             own_spec(video_here),
@@ -777,11 +851,12 @@
             weight_spec(1),
             weight_spec(2),
             row_spec,
+            item_spec(keys_here),
         ],
         [
             item_out(lat_rows, BF16),
-            item_out(keys_here, BF16),
-            item_out(keys_here, BF16),
+            (pl.BlockSpec((2 * PAIR, D), lambda i, s: (0, 0)), (2 * PAIR, D), F32),
+            (pl.BlockSpec((2 * PAIR, D), lambda i, s: (0, 0)), (2 * PAIR, D), F32),
             (own_spec(video_here), video_tokens.shape, F32),
             item_out(video_here, BF16),
             item_out(cap_rows, BF16),
@@ -789,9 +864,13 @@
         ],
         (
             queries, keys, values, lse, attended, d_att, video_tokens, video_other, cap, mask,
-            weights, weights, gain_tok_row,
+            weights, weights, gain_tok_row, tok_norm,
         ),
-    )
+        58,
+        [pltpu.VMEM((keys_here, D), BF16), pltpu.VMEM((keys_here, D), BF16)],
+    )
+    growth, d_queries = lax.optimization_barrier((growth, d_queries))
+    out_mine = (after_attn + growth.astype(F32)).astype(BF16)
     other_here = swap_cores(other_back)
     (video_grad,) = call(
         place_kernel,
@@ -805,6 +884,7 @@
             )
         ],
         (video_grad, other_here),
+        6,
         aliases={1: 0},
     )
     caption_grad = jnp.zeros((txt_count, own, cap_here, D), F32)
@@ -819,26 +899,33 @@
     caption_grad = caption_grad.reshape(caption_tokens.shape)
 
     d_lat_norm = dot("ble,ed->bld", d_queries, w_query)
-    d_lat_back, gain_lat_part = norm_back_rows(lat.astype(F32), gain_latent, d_lat_norm)
+    d_lat_back, gain_lat_part = norm_back_rows(lat_float, gain_latent, d_lat_norm)
     lat_grad_mine = d_after + d_lat_back
 
     def mine_cols(array):
         return lax.dynamic_slice_in_dim(array, z * head_width, head_width, array.ndim - 1)
 
+    def mine_rows(rows):
+        return lax.dynamic_slice_in_dim(rows, z * head_width - window, head_width, 0)
+
+    grad_up, grad_down = lax.psum((grad_up.astype(BF16), grad_down.astype(BF16)), ("vid", "txt"))
     grad_out = dot("ble,bld->ed", mine_cols(mixed_in), d_branch)
-    grad_query = dot("bld,ble->de", lat_norm, mine_cols(d_queries))
-    grad_key = dot("bld,ble->de", tok_norm, mine_cols(d_keys))
-    grad_value = dot("bld,ble->de", tok_norm, mine_cols(d_values))
-    extra = jnp.zeros((8, D), F32)
-    extra = extra.at[0].set(jnp.sum(gain_mlp_part, axis=0)).at[1].set(jnp.sum(keep))
-    grad_up, grad_down, out_rows = lax.psum(
-        (grad_up, grad_down, jnp.concatenate([grad_out, extra])), ("vid", "txt")
-    )
-    gains = jnp.stack([jnp.sum(gain_lat_part, axis=0), gain_tok_part[0]])
-    gains = gains.reshape(2 * D // head_width, head_width)
-    late = jnp.concatenate([grad_query, grad_key, grad_value, gains])
-    late = lax.psum(late.astype(BF16), ("vid", "txt")).astype(F32)
-    gains = late[3 * D :].reshape(2, D)
+    grad_query = dot("ble,bld->ed", mine_cols(d_queries), lat_norm)
+    gains = jnp.stack(
+        [
+            jnp.sum(gain_lat_part, axis=0),
+            gain_tok_part[0],
+            jnp.sum(gain_mlp_part, axis=0),
+            jnp.full((D,), jnp.sum(keep)),
+        ]
+    )
+    count = 4 * head_width + gains.shape[0]
+    spare = jnp.zeros((-count % (32 * txt_count), D), F32)
+    late = jnp.concatenate(
+        [grad_query, mine_rows(key_rows), mine_rows(value_rows), grad_out, gains, spare]
+    )
+    late = sum_over_group(late, core, place, txt_count).astype(F32)
+    gains = late[4 * head_width :]
 
     def give_back(values):
         other = swap_cores(values[:, lat_half:].astype(BF16)).astype(values.dtype)
@@ -848,21 +935,21 @@
 
     latents_out = give_back(out_mine)
     latent_grad = give_back(lat_grad_mine)
-    kept_count = out_rows[head_width + 1, 0].astype(jnp.int32)
+    kept_count = gains[3, 0].astype(jnp.int32)
     return (
         latents_out,
         latent_grad,
         video_grad,
         caption_grad,
-        late[:D],
-        late[D : 2 * D],
-        late[2 * D : 3 * D],
-        out_rows[:head_width],
-        grad_up,
-        grad_down,
+        late[:head_width].T,
+        late[head_width : 2 * head_width].T,
+        late[2 * head_width : 3 * head_width].T,
+        late[3 * head_width : 4 * head_width],
+        grad_up.astype(F32),
+        grad_down.astype(F32),
         gains[0],
         gains[1],
-        out_rows[head_width],
+        gains[2],
         kept_count,
     )
 

time: 509 us -> 397 us (0.78)
  waiting for transfers between devices: 228 us -> 83.9 us
  starting transfers between devices: 33.5 us -> 56.8 us
  matrix products: 38.7 us -> 22.7 us
  Pallas kernels: 120 us -> 132 us
  local copies, waits for them, and re-layouts: 47.9 us -> 57 us
    psum x2 -> x1, waiting for transfers between devices: 127 us -> 4.67 us  [local(): lax.psum((grad_up.astype(BF16), grad_down.astype(BF16)), ('vid', 'txt'))]
    ppermute x0 -> x12, waiting for transfers between devices: none -> 46.9 us  [the longest x1 19.2 us: local(): down2 = lax.ppermute(down1, 'head', [(1, 0), (2, 1)])]
    ppermute x9 -> x6, waiting for transfers between devices: 65.7 us -> 28.9 us  [head_shift(): lax.ppermute(values, 'head', [(i, (i - shift) % count) for i in range(cou...]
    psum x1, waiting for transfers between devices: 32.5 us -> 0.01 us  [local(): lax.psum(dot('blf,fd->bld', activ, down_weight).astype(BF16), 'head')]
    ppermute x0 -> x12, starting transfers between devices: none -> 24.3 us  [the longest x1 7.33 us: local(): up3 = lax.ppermute(half_then, 'head', [(0, 3)])]
    dot_general x12 -> x11, matrix products: 38.7 us -> 22.7 us  [dot(): return jnp.einsum(spec, a, b, preferred_element_type=F32)]
    pallas_call x4 -> x5, Pallas kernels: 120 us -> 132 us  [call(): pl.pallas_call(kernel, name=name, grid_spec=pltpu.PrefetchScalarGridSpec(...]
    concatenate x0 -> x1, local copies, waits for them, and re-layouts: none -> 11.4 us  [local(): jnp.concatenate([grad_query, mine_rows(key_rows), mine_rows(value_rows),...]
  transfers between devices with their start and end apart: 26 -> 37, of which waited for: 10 -> 14; matrix products, arithmetic and copies ran while one was open for 12% -> 22% of each run, Pallas kernels for 0% -> 16%
where the time goes in v2:
time: 397 us; the launch traced here: 395 us
  Pallas kernels  132 us (33%)
  waiting for transfers between devices  83.9 us (21%)
  local copies, waits for them, and re-layouts  57 us (14%)
  starting transfers between devices  56.8 us (14%)
  other arithmetic  25.9 us (7%)
  matrix products  22.7 us (6%)
  between operations  16.8 us (4%)
    pallas_call x5, Pallas kernels, call(): pl.pallas_call(kernel, name=name, grid_spec=pltpu.PrefetchScalarGridSpec(...  132 us
    ppermute x6, waiting for transfers between devices, head_shift(): lax.ppermute(values, 'head', [(i, (i - shift) % count) for i in range(cou...  28.9 us
    dot_general x11, matrix products, dot(): return jnp.einsum(spec, a, b, preferred_element_type=F32)  22.7 us
    ppermute x1, waiting for transfers between devices, local(): down2 = lax.ppermute(down1, 'head', [(1, 0), (2, 1)])  19.2 us
    ppermute x4, starting transfers between devices, local(): lax.ppermute(cap_back[:, step * cap_here:(step + 1) * cap_here], ('vid',...  11.9 us
    ppermute x3, waiting for transfers between devices, sum_over_group(): lax.ppermute(total, 'txt', perm)  11.5 us
    concatenate x1, local copies, waits for them, and re-layouts, local(): jnp.concatenate([grad_query, mine_rows(key_rows), mine_rows(value_rows),...  11.4 us
    ppermute x3, waiting for transfers between devices, sum_over_group(): total = total + lax.ppermute(chunk, 'txt', perm).astype(F32)  10.6 us
  transfers between devices with their start and end apart: 37, of which 14 were waited for; matrix products, arithmetic and copies ran while one was open for 22% of the time, Pallas kernels for 16%

profile of v2, /device:TPU:0, one launch (start us, length us, event | category | flops | bytes accessed | tf_op | source)
XLA Modules:
  0.0 395.0 jit_solution(2957501091397263586)
XLA Ops:
  9.6 5.0 %collective-permute-start.6 = (bf16[2,192,768]{2,1,0:T(8,128)(2,1)}, bf16[2,192,768]{2,1,0:T(8,128)(2,1)S(1)}, u32[]{:S(2)}, u32[]{:S(2)}) collective-permute-start(bf16[2,192,768]{2,1,0:T(8,128)(2,1)} %constant_dynamic-slice_fusion.6), channel_id=1, source_target_pairs={{0,1},{1,2},{2,3},{4,5},{5,6},{6,7},{8,9},{9,10},{10,11},{12,13},{... | collective-permute-start | bytes 1769480 | tf_op jit(solution)/shard_map/ppermute | solution.py:669
  41.7 3.2 collective-permute-done.3
  47.5 7.3 %collective-permute-start.10 = (bf16[2,192,768]{2,1,0:T(8,128)(2,1)}, bf16[2,192,768]{2,1,0:T(8,128)(2,1)S(1)}, u32[]{:S(2)}, u32[]{:S(2)}) collective-permute-start(bf16[2,192,768]{2,1,0:T(8,128)(2,1)} %constant_dynamic-slice_fusion.6), channel_id=1, source_target_pairs={{0,3},{4,7},{8,11},{12,15},{16,19},{20,23},{24,27},{28,31}} | collective-permute-start | bytes 1769480 | tf_op jit(solution)/shard_map/ppermute | solution.py:688
  62.8 5.7 %collective-permute-done.10 = bf16[2,192,768]{2,1,0:T(8,128)(2,1)S(1)} collective-permute-done((bf16[2,192,768]{2,1,0:T(8,128)(2,1)}, bf16[2,192,768]{2,1,0:T(8,128)(2,1)S(1)}, u32[]{:S(2)}, u32[]{:S(2)}) %collective-permute-start.10) | collective-permute-done | bytes 589856 | tf_op jit(solution)/shard_map/ppermute | solution.py:688
  68.4 19.2 %collective-permute-done.8 = bf16[2,192,768]{2,1,0:T(8,128)(2,1)S(1)} collective-permute-done((bf16[2,192,768]{2,1,0:T(8,128)(2,1)}, bf16[2,192,768]{2,1,0:T(8,128)(2,1)S(1)}, u32[]{:S(2)}, u32[]{:S(2)}) %collective-permute-start.8) | collective-permute-done | bytes 589856 | tf_op jit(solution)/shard_map/ppermute | solution.py:687
  97.2 10.3 %token_norm.1 = (bf16[4,1088,768]{2,1,0:T(8,128)(2,1)}, bf16[4,128,768]{2,1,0:T(8,128)(2,1)}) custom-call(s32[3]{0:T(128)} %add_add_fusion.1.s_ref, bf16[8,512,768]{2,1,0:T(8,128)(2,1)} %own_ref.3, bf16[4,512,768]{2,1,0:T(8,128)(2,1)} %collective-permute-done.1.other_ref, bf16[4,64,768]{2,1,0:T(8,128)(2,1)} %pad_maximum_fusion.4.cap_ref, ...), custom_call_target="tpu_custom_call" | custom-call | flops 9900000256 | bytes 9000000 | tf_op jit(solution)/shard_map/token_norm/pallas_call | solution.py:756
  108.3 26.5 %attention_forward.2 = (bf16[4,128,768]{2,1,0:T(8,128)(2,1)}, bf16[4,1088,768]{2,1,0:T(8,128)(2,1)}, bf16[4,1088,768]{2,1,0:T(8,128)(2,1)}, f32[4,2,8,256]{3,2,1,0:T(8,128)}, f32[4,128,768]{2,1,0:T(8,128)}) custom-call(s32[3]{0:T(128)} %add_add_fusion.1.s_ref, bf16[4,1088,768]{2,1,0:T(8,128)(2,1)} %get-tuple-element.52.tok_ref, ...), custom_call_target="tpu_custom_call" | custom-call | flops 25300000768 | bytes 23000000 | tf_op jit(solution)/shard_map/attention_forward/pallas_call | solution.py:756
  134.8 26.5 %attention_forward.3 = (bf16[4,128,768]{2,1,0:T(8,128)(2,1)}, bf16[4,1088,768]{2,1,0:T(8,128)(2,1)}, bf16[4,1088,768]{2,1,0:T(8,128)(2,1)}, f32[4,2,8,256]{3,2,1,0:T(8,128)}, f32[4,128,768]{2,1,0:T(8,128)}) custom-call(s32[3]{0:T(128)} %add_add_fusion.s_ref, ...), custom_call_target="tpu_custom_call", output_to_operand_aliasing={{0}: (7, {}), {1}: (8, {}), {2}: (9, {}), {3}: (10, {}), {4... | custom-call | flops 25300000768 | bytes 23000000 | tf_op jit(solution)/shard_map/attention_forward/pallas_call | solution.py:756
  164.5 3.9 multiply_convert_fusion.1
  174.6 5.6 %collective-permute-done.16 = bf16[128,768]{1,0:T(8,128)(2,1)S(1)} collective-permute-done((bf16[128,768]{1,0:T(8,128)(2,1)S(1)}, bf16[128,768]{1,0:T(8,128)(2,1)S(1)}, u32[]{:S(2)}, u32[]{:S(2)}) %collective-permute-start.16) | collective-permute-done | bytes 196640 | tf_op jit(solution)/shard_map/ppermute | solution.py:396
  180.2 7.8 %collective-permute-done.15 = bf16[128,768]{1,0:T(8,128)(2,1)S(1)} collective-permute-done((bf16[128,768]{1,0:T(8,128)(2,1)S(1)}, bf16[128,768]{1,0:T(8,128)(2,1)S(1)}, u32[]{:S(2)}, u32[]{:S(2)}) %collective-permute-start.15) | collective-permute-done | bytes 196640 | tf_op jit(solution)/shard_map/ppermute | solution.py:396
  188.2 4.9 %collective-permute-start.17 = (bf16[128,768]{1,0:T(8,128)(2,1)S(1)}, bf16[128,768]{1,0:T(8,128)(2,1)S(1)}, u32[]{:S(2)}, u32[]{:S(2)}) collective-permute-start(bf16[128,768]{1,0:T(8,128)(2,1)S(1)} %get-tuple-element.96), channel_id=1, source_target_pairs={{0,3},{1,0},{2,1},{3,2},{4,7},{5,4},{6,5},{7,6},{8,11},{9,8},{10,9... | collective-permute-start | bytes 589832 | tf_op jit(solution)/shard_map/ppermute | solution.py:396
  198.3 13.8 %collective-permute-done.18 = bf16[128,768]{1,0:T(8,128)(2,1)S(1)} collective-permute-done((bf16[128,768]{1,0:T(8,128)(2,1)S(1)}, bf16[128,768]{1,0:T(8,128)(2,1)S(1)}, u32[]{:S(2)}, u32[]{:S(2)}) %collective-permute-start.18) | collective-permute-done | bytes 196640 | tf_op jit(solution)/shard_map/ppermute | solution.py:396
  218.0 62.7 %attention_backward.1 = (bf16[4,128,768]{2,1,0:T(8,128)(2,1)}, f32[256,768]{1,0:T(8,128)}, f32[256,768]{1,0:T(8,128)}, f32[8,512,768]{2,1,0:T(8,128)}, bf16[4,51...) custom-call(s32[3]{0:T(128)} %add_add_fusion.1.s_ref, ...), custom_call_target="tpu_custom_call" | custom-call | flops 63800000512 | bytes 58000000 | tf_op jit(solution)/shard_map/attention_backward/pallas_call | solution.py:756
  284.7 5.5 %collective-permute-start.24 = (bf16[4,16,768]{2,1,0:T(8,128)(2,1)}, bf16[4,16,768]{2,1,0:T(8,128)(2,1)}, u32[]{:S(2)}, u32[]{:S(2)}) collective-permute-start(bf16[4,16,768]{2,1,0:T(8,128)(2,1)} %get-tuple-element.126), channel_id=1, source_target_pairs={{16,0},{4,4},{20,8},{0,12},{24,16},{12,20},{28,24},{8,28},{17,1},{... | collective-permute-start | bytes 294920 | tf_op jit(solution)/shard_map/ppermute | solution.py:893
  290.2 4.2 %collective-permute-start.26 = (bf16[4,16,768]{2,1,0:T(8,128)(2,1)}, bf16[4,16,768]{2,1,0:T(8,128)(2,1)}, u32[]{:S(2)}, u32[]{:S(2)}) collective-permute-start(bf16[4,16,768]{2,1,0:T(8,128)(2,1)} %get-tuple-element.124), channel_id=1, source_target_pairs={{20,0},{0,4},{16,8},{4,12},{28,16},{8,20},{24,24},{12,28},{21,1},{... | collective-permute-start | bytes 294920 | tf_op jit(solution)/shard_map/ppermute | solution.py:893
  312.3 3.8 fusion.12
  318.2 11.4 %concatenate.45 = f32[896,768]{1,0:T(8,128)} concatenate(f32[192,768]{1,0:T(8,128)} %convolution_bitcast_fusion.1, f32[192,768]{1,0:T(8,128)S(1)} %constant_dynamic-slice_fusion.5, f32[192,768]{1,0:T(8,128)S(1)} %constant_dynamic-slice_fusion.4, f32[192,768]{1,0:T(8,128)} %convolution_bitcast_fusion, f32[1,768]{1,0:T(1,128)S(1)} %stack.64, f32[1,768]{1,0:T(1,128)} %slice.144, ...), dimensions={0} | concatenate | bytes 5505024 | tf_op jit(solution)/shard_map/concatenate | solution.py:924
  336.5 7.9 %collective-permute-done.30 = bf16[112,768]{1,0:T(8,128)(2,1)S(1)} collective-permute-done((bf16[112,768]{1,0:T(8,128)(2,1)S(1)}, bf16[112,768]{1,0:T(8,128)(2,1)S(1)}, u32[]{:S(2)}, u32[]{:S(2)}) %collective-permute-start.30) | collective-permute-done | bytes 172064 | tf_op jit(solution)/shard_map/ppermute | solution.py:428
  344.4 2.8 collective-permute-done.29
  355.3 8.7 %collective-permute-done.33 = bf16[112,768]{1,0:T(8,128)(2,1)S(1)} collective-permute-done((bf16[112,768]{1,0:T(8,128)(2,1)S(1)}, bf16[112,768]{1,0:T(8,128)(2,1)S(1)}, u32[]{:S(2)}, u32[]{:S(2)}) %collective-permute-start.33) | collective-permute-done | bytes 172064 | tf_op jit(solution)/shard_map/ppermute | solution.py:434
  364.3 4.7 %all-reduce.7.cloned.1.call-done = (bf16[768,768]{1,0:T(8,128)(2,1)}, bf16[768,768]{1,0:T(8,128)(2,1)}) async-done(((bf16[768,768]{1,0:T(8,128)(2,1)}, bf16[768,768]{1,0:T(8,128)(2,1)}), (bf16[768,768]{1,0:T(8,128)(2,1)}, bf16[768,768]{1,0:T(8,128)(2,1)})) %all-reduce.7.cloned.1.call-update) | async-done | bytes 2359312 | tf_op jit(solution)/shard_map/psum | solution.py:911
  369.0 2.9 convert_element_type.141
  381.2 5.8 %place_rows.1 = f32[8,512,768]{2,1,0:T(8,128)} custom-call(s32[3]{0:T(128)} %add_add_fusion.1.s_ref, f32[8,512,768]{2,1,0:T(8,128)} %get-tuple-element.72.whole_ref, bf16[4,512,768]{2,1,0:T(8,128)(2,1)} %collective-permute-done.22.part_ref), custom_call_target="tpu_custom_call", output_to_operand_aliasing={{}: (1, {})} | custom-call | flops 6600000000 | bytes 6000000 | tf_op jit(solution)/shard_map/place_rows/pallas_call | solution.py:756
  (261 shorter events, 118.2 us)
Async XLA Ops:
  7.2 302.4 %all-reduce.5.cloned.1.call-start = ((), (), s32[]{:S(2)}) async-start(), calls=%async_computation | async-start | bytes 1572864 | tf_op jit(solution)/shard_map/psum | solution.py:829
  9.6 37.9 %collective-permute-start.6 = (bf16[2,192,768]{2,1,0:T(8,128)(2,1)}, bf16[2,192,768]{2,1,0:T(8,128)(2,1)S(1)}, u32[]{:S(2)}, u32[]{:S(2)}) collective-permute-start(bf16[2,192,768]{2,1,0:T(8,128)(2,1)} %constant_dynamic-slice_fusion.6), channel_id=1, source_target_pairs={{0,1},{1,2},{2,3},{4,5},{5,6},{6,7},{8,9},{9,10},{10,11},{12,13},{... | collective-permute-start | bytes 1769480 | tf_op jit(solution)/shard_map/ppermute | solution.py:669
  14.6 32.9 %collective-permute-start.7 = (bf16[2,192,768]{2,1,0:T(8,128)(2,1)}, bf16[2,192,768]{2,1,0:T(8,128)(2,1)}, u32[]{:S(2)}, u32[]{:S(2)}) collective-permute-start(bf16[2,192,768]{2,1,0:T(8,128)(2,1)} %constant_dynamic-slice_fusion.6), channel_id=1, source_target_pairs={{1,0},{2,1},{3,2},{5,4},{6,5},{7,6},{9,8},{10,9},{11,10},{13,12},{... | collective-permute-start | bytes 1769480 | tf_op jit(solution)/shard_map/ppermute | solution.py:670
  17.0 20.0 %collective-permute-start.5 = (bf16[4,17,768]{2,1,0:T(8,128)(2,1)}, bf16[4,17,768]{2,1,0:T(8,128)(2,1)}, u32[]{:S(2)}, u32[]{:S(2)}) collective-permute-start(bf16[4,17,768]{2,1,0:T(8,128)(2,1)} %get-tuple-element.123), channel_id=1, source_target_pairs={{0,20},{4,0},{8,16},{12,4},{16,28},{20,8},{24,24},{28,12},{1,21},{... | collective-permute-start | bytes 313352 | tf_op jit(solution)/shard_map/ppermute | solution.py:724
  19.5 19.4 %collective-permute-start.4 = (bf16[4,17,768]{2,1,0:T(8,128)(2,1)}, bf16[4,17,768]{2,1,0:T(8,128)(2,1)}, u32[]{:S(2)}, u32[]{:S(2)}) collective-permute-start(bf16[4,17,768]{2,1,0:T(8,128)(2,1)} %get-tuple-element.122), channel_id=1, source_target_pairs={{0,4},{4,20},{8,0},{12,16},{16,12},{20,28},{24,8},{28,24},{1,5},{5... | collective-permute-start | bytes 313352 | tf_op jit(solution)/shard_map/ppermute | solution.py:724
  27.1 31.1 %collective-permute-start = (bf16[4,128,768]{2,1,0:T(8,128)(2,1)}, bf16[4,128,768]{2,1,0:T(8,128)(2,1)}, u32[]{:S(2)}, u32[]{:S(2)}) collective-permute-start(bf16[4,128,768]{2,1,0:T(8,128)(2,1)} %constant_dynamic-slice_fusion.8), channel_id=1, source_target_pairs={{0,16},{16,0},{1,17},{17,1},{2,18},{18,2},{3,19},{19,3},{4,20},{20... | collective-permute-start | bytes 2359304 | tf_op jit(solution)/shard_map/ppermute | solution.py:392
  47.5 20.9 %collective-permute-start.10 = (bf16[2,192,768]{2,1,0:T(8,128)(2,1)}, bf16[2,192,768]{2,1,0:T(8,128)(2,1)S(1)}, u32[]{:S(2)}, u32[]{:S(2)}) collective-permute-start(bf16[2,192,768]{2,1,0:T(8,128)(2,1)} %constant_dynamic-slice_fusion.6), channel_id=1, source_target_pairs={{0,3},{4,7},{8,11},{12,15},{16,19},{20,23},{24,27},{28,31}} | collective-permute-start | bytes 1769480 | tf_op jit(solution)/shard_map/ppermute | solution.py:688
  54.9 32.7 %collective-permute-start.11 = (bf16[2,192,768]{2,1,0:T(8,128)(2,1)}, bf16[2,192,768]{2,1,0:T(8,128)(2,1)S(1)}, u32[]{:S(2)}, u32[]{:S(2)}) collective-permute-start(bf16[2,192,768]{2,1,0:T(8,128)(2,1)} %constant_dynamic-slice_fusion.6), channel_id=1, source_target_pairs={{3,0},{7,4},{11,8},{15,12},{19,16},{23,20},{27,24},{31,28}} | collective-permute-start | bytes 1769480 | tf_op jit(solution)/shard_map/ppermute | solution.py:689
  56.9 30.7 %collective-permute-start.8 = (bf16[2,192,768]{2,1,0:T(8,128)(2,1)}, bf16[2,192,768]{2,1,0:T(8,128)(2,1)S(1)}, u32[]{:S(2)}, u32[]{:S(2)}) collective-permute-start(bf16[2,192,768]{2,1,0:T(8,128)(2,1)} %collective-permute-done.7), channel_id=1, source_target_pairs={{1,0},{2,1},{5,4},{6,5},{9,8},{10,9},{13,12},{14,13},{17,16},{18,1... | collective-permute-start | bytes 1769480 | tf_op jit(solution)/shard_map/ppermute | solution.py:687
  58.2 39.0 %collective-permute-start.1 = (bf16[4,512,768]{2,1,0:T(8,128)(2,1)S(1)}, bf16[4,512,768]{2,1,0:T(8,128)(2,1)}, u32[]{:S(2)}, u32[]{:S(2)}) collective-permute-start(bf16[4,512,768]{2,1,0:T(8,128)(2,1)S(1)} %constant_dynamic-slice_fusion.7), channel_id=1, source_target_pairs={{0,16},{16,0},{1,17},{17,1},{2,18},{18,2},{3,19},{19,3},{4,20},{20... | collective-permute-start | bytes 9437192 | tf_op jit(solution)/shard_map/ppermute | solution.py:392
  62.7 27.2 %collective-permute-start.13 = (bf16[2,192,768]{2,1,0:T(8,128)(2,1)S(1)}, bf16[2,192,768]{2,1,0:T(8,128)(2,1)S(1)}, u32[]{:S(2)}, u32[]{:S(2)}) collective-permute-start(bf16[2,192,768]{2,1,0:T(8,128)(2,1)S(1)} %get-tuple-element.100), channel_id=1, source_target_pairs={{0,16},{16,0},{1,17},{17,1},{2,18},{18,2},{3,19},{19,3},{4,20},{20... | collective-permute-start | bytes 1769480 | tf_op jit(solution)/shard_map/ppermute | solution.py:392
  172.2 15.8 %collective-permute-start.15 = (bf16[128,768]{1,0:T(8,128)(2,1)S(1)}, bf16[128,768]{1,0:T(8,128)(2,1)S(1)}, u32[]{:S(2)}, u32[]{:S(2)}) collective-permute-start(bf16[128,768]{1,0:T(8,128)(2,1)S(1)} %get-tuple-element.114), channel_id=1, source_target_pairs={{0,2},{1,3},{2,0},{3,1},{4,6},{5,7},{6,4},{7,5},{8,10},{9,11},{10,... | collective-permute-start | bytes 589832 | tf_op jit(solution)/shard_map/ppermute | solution.py:396
  172.2 15.8 %collective-permute-start.14 = (bf16[128,768]{1,0:T(8,128)(2,1)S(1)}, bf16[128,768]{1,0:T(8,128)(2,1)S(1)}, u32[]{:S(2)}, u32[]{:S(2)}) collective-permute-start(bf16[128,768]{1,0:T(8,128)(2,1)S(1)} %get-tuple-element.112), channel_id=1, source_target_pairs={{0,3},{1,0},{2,1},{3,2},{4,7},{5,4},{6,5},{7,6},{8,11},{9,8},{10,9... | collective-permute-start | bytes 589832 | tf_op jit(solution)/shard_map/ppermute | solution.py:396
  195.0 17.1 %collective-permute-start.18 = (bf16[128,768]{1,0:T(8,128)(2,1)S(1)}, bf16[128,768]{1,0:T(8,128)(2,1)S(1)}, u32[]{:S(2)}, u32[]{:S(2)}) collective-permute-start(bf16[128,768]{1,0:T(8,128)(2,1)S(1)} %get-tuple-element.96), channel_id=1, source_target_pairs={{0,2},{1,3},{2,0},{3,1},{4,6},{5,7},{6,4},{7,5},{8,10},{9,11},{10,... | collective-permute-start | bytes 589832 | tf_op jit(solution)/shard_map/ppermute | solution.py:396
  196.6 15.5 %collective-permute-start.19 = (bf16[128,768]{1,0:T(8,128)(2,1)S(1)}, bf16[128,768]{1,0:T(8,128)(2,1)S(1)}, u32[]{:S(2)}, u32[]{:S(2)}) collective-permute-start(bf16[128,768]{1,0:T(8,128)(2,1)S(1)} %get-tuple-element.96), channel_id=1, source_target_pairs={{0,1},{1,2},{2,3},{3,0},{4,5},{5,6},{6,7},{7,4},{8,9},{9,10},{10,1... | collective-permute-start | bytes 589832 | tf_op jit(solution)/shard_map/ppermute | solution.py:396
  213.9 155.1 %all-reduce.7.cloned.1.call-start = ((), (), s32[]{:S(2)}) async-start(), calls=%async_computation.1 | async-start | bytes 4718592 | tf_op jit(solution)/shard_map/psum | solution.py:911
  280.7 100.5 %collective-permute-start.22 = (bf16[4,512,768]{2,1,0:T(8,128)(2,1)}, bf16[4,512,768]{2,1,0:T(8,128)(2,1)}, u32[]{:S(2)}, u32[]{:S(2)}) collective-permute-start(bf16[4,512,768]{2,1,0:T(8,128)(2,1)} %get-tuple-element.73), channel_id=1, source_target_pairs={{0,16},{16,0},{1,17},{17,1},{2,18},{18,2},{3,19},{19,3},{4,20},{20... | collective-permute-start | bytes 9437192 | tf_op jit(solution)/shard_map/ppermute | solution.py:392
  282.5 19.7 %collective-permute-start.23 = (bf16[4,16,768]{2,1,0:T(8,128)(2,1)}, bf16[4,16,768]{2,1,0:T(8,128)(2,1)}, u32[]{:S(2)}, u32[]{:S(2)}) collective-permute-start(bf16[4,16,768]{2,1,0:T(8,128)(2,1)} %get-tuple-element.127), channel_id=1, source_target_pairs={{0,0},{16,4},{4,8},{20,12},{8,16},{24,20},{12,24},{28,28},{1,1},{1... | collective-permute-start | bytes 294920 | tf_op jit(solution)/shard_map/ppermute | solution.py:893
  284.7 20.2 %collective-permute-start.24 = (bf16[4,16,768]{2,1,0:T(8,128)(2,1)}, bf16[4,16,768]{2,1,0:T(8,128)(2,1)}, u32[]{:S(2)}, u32[]{:S(2)}) collective-permute-start(bf16[4,16,768]{2,1,0:T(8,128)(2,1)} %get-tuple-element.126), channel_id=1, source_target_pairs={{16,0},{4,4},{20,8},{0,12},{24,16},{12,20},{28,24},{8,28},{17,1},{... | collective-permute-start | bytes 294920 | tf_op jit(solution)/shard_map/ppermute | solution.py:893
  290.2 16.3 %collective-permute-start.25 = (bf16[4,16,768]{2,1,0:T(8,128)(2,1)}, bf16[4,16,768]{2,1,0:T(8,128)(2,1)}, u32[]{:S(2)}, u32[]{:S(2)}) collective-permute-start(bf16[4,16,768]{2,1,0:T(8,128)(2,1)} %get-tuple-element.125), channel_id=1, source_target_pairs={{4,0},{20,4},{0,8},{16,12},{12,16},{28,20},{8,24},{24,28},{5,1},{2... | collective-permute-start | bytes 294920 | tf_op jit(solution)/shard_map/ppermute | solution.py:893
  290.2 17.8 %collective-permute-start.26 = (bf16[4,16,768]{2,1,0:T(8,128)(2,1)}, bf16[4,16,768]{2,1,0:T(8,128)(2,1)}, u32[]{:S(2)}, u32[]{:S(2)}) collective-permute-start(bf16[4,16,768]{2,1,0:T(8,128)(2,1)} %get-tuple-element.124), channel_id=1, source_target_pairs={{20,0},{0,4},{16,8},{4,12},{28,16},{8,20},{24,24},{12,28},{21,1},{... | collective-permute-start | bytes 294920 | tf_op jit(solution)/shard_map/ppermute | solution.py:893
  332.3 41.3 %collective-permute-start.20 = (bf16[4,64,768]{2,1,0:T(8,128)(2,1)}, bf16[4,64,768]{2,1,0:T(8,128)(2,1)}, u32[]{:S(2)}, u32[]{:S(2)}) collective-permute-start(bf16[4,64,768]{2,1,0:T(8,128)(2,1)} %get-tuple-element.110), channel_id=1, source_target_pairs={{0,16},{16,0},{1,17},{17,1},{2,18},{18,2},{3,19},{19,3},{4,20},{20... | collective-permute-start | bytes 1179656 | tf_op jit(solution)/shard_map/ppermute | solution.py:392
  333.8 13.3 %collective-permute-start.29 = (bf16[112,768]{1,0:T(8,128)(2,1)S(1)}, bf16[112,768]{1,0:T(8,128)(2,1)S(1)}, u32[]{:S(2)}, u32[]{:S(2)}) collective-permute-start(bf16[112,768]{1,0:T(8,128)(2,1)S(1)} %get-tuple-element.119), channel_id=1, source_target_pairs={{0,8},{4,12},{8,0},{12,4},{1,9},{5,13},{9,1},{13,5},{2,10},{6,14},... | collective-permute-start | bytes 516104 | tf_op jit(solution)/shard_map/ppermute | solution.py:428
  350.6 24.0 %collective-permute-start.21 = (bf16[4,64,768]{2,1,0:T(8,128)(2,1)S(1)}, bf16[4,64,768]{2,1,0:T(8,128)(2,1)}, u32[]{:S(2)}, u32[]{:S(2)}) collective-permute-start(bf16[4,64,768]{2,1,0:T(8,128)(2,1)S(1)} %slice.186), channel_id=1, source_target_pairs={{0,16},{16,0},{1,17},{17,1},{2,18},{18,2},{3,19},{19,3},{4,20},{20... | collective-permute-start | bytes 1179656 | tf_op jit(solution)/shard_map/ppermute | solution.py:392
  (56 other events, 972.0 us)
Sparse Core Ops, SparseCore 0:
  214.0 43.0 all-reduce.4
  301.2 67.7 all-reduce.6
